TPU v7x, 256 devices: a whole 4x4x8 slice. The times are simulated.
256 devices in a mesh: rows: 32 (over y_lo, z, core), protos: 8 (over y_hi, x).
Axes of the slice: x: 4, y: 4 (y_hi: 2, y_lo: 2; y = y_hi * 2 + y_lo), z: 8, core: 2. Of those that a mesh axis runs over, the one named last changes fastest.
Arguments:
- teacher: bfloat16 [2048, 256], P('rows')
- students: bfloat16 [8192, 256], P('rows')
- prototypes: bfloat16 [256, 65536], P(None, 'protos')
- pairing: int32 [8192], P('rows'), may hold values from 0 to 63
- layout: int32 [8192], P('rows'), may hold values from 0 to 31, as said below
Outputs:
- grad_students: float32 [8192, 256], P('rows')
- grad_protos: float32 [256, 65536], P('rows', 'protos')
Inputs may be any that keep to these rules, and one draw needn't show every extreme that they name: `layout`: in each aligned block of 256 rows, every value appears exactly 8 times.
All inputs are finite; a program needn't handle non-finite values.
Results may differ from a plain program's by a relative error of at most 0.0003.
The roundings to bfloat16 on the way count: a program that leaves them out, or rounds other values in their place, can miss the bound.
Values may be sent and summed in bfloat16 or wider, within the bound.
A program may use at most 64 MiB of HBM per device.

v0:
```python
import jax
import jax.numpy as jnp
from jax import lax
from jax.sharding import PartitionSpec as P

PROTOS = 65536
ITERS = 2


epsilon = 1e-06
teacher_temp = 0.07
student_temp = 0.1
loss_scale = 16.0


def body(teacher, students, prototypes, pairing, layout):
    row_devices = lax.axis_size("rows")
    tea_count = teacher.shape[0]
    total_teachers = tea_count * row_devices
    local_protos = prototypes.shape[1]
    weights = prototypes.astype(jnp.float32)
    w_norm = jnp.sqrt(jnp.sum(weights * weights, 0) + epsilon)
    w_unit = weights / w_norm
    w_unit_b = w_unit.astype(jnp.bfloat16)
    tea_full = teacher.astype(jnp.float32)
    tea_unit_b = (
        tea_full / jnp.sqrt(jnp.sum(tea_full * tea_full, 1, keepdims=True) + epsilon)
    ).astype(jnp.bfloat16)
    exp_scores = jnp.exp(
        jnp.dot(tea_unit_b, w_unit_b, preferred_element_type=jnp.float32) / teacher_temp
    )
    row_factor = jnp.ones((tea_count,), jnp.float32)
    col_factor = jnp.ones((local_protos,), jnp.float32)
    for sweep in range(ITERS):
        colsum = lax.psum(jnp.sum(exp_scores * row_factor[:, None], 0), "rows")
        col_factor = 1.0 / (PROTOS * colsum)
        rowsum = lax.psum(jnp.sum(exp_scores * col_factor[None, :], 1), "protos")
        row_factor = 1.0 / (total_teachers * rowsum)
    send_order = jnp.argsort(layout, stable=True)
    moved_rows, moved_pairs = (
        lax.all_to_all(students[send_order], "rows", split_axis=0, concat_axis=0, tiled=True),
        lax.all_to_all(pairing[send_order], "rows", split_axis=0, concat_axis=0, tiled=True),
    )
    balanced = total_teachers * exp_scores * row_factor[:, None] * col_factor[None, :]
    target_rows = balanced[moved_pairs]
    stu_full = moved_rows.astype(jnp.float32)
    u_norm = jnp.sqrt(jnp.sum(stu_full * stu_full, 1, keepdims=True) + epsilon)
    stu_unit = stu_full / u_norm
    stu_unit_b = stu_unit.astype(jnp.bfloat16)
    logits = jnp.dot(stu_unit_b, w_unit_b, preferred_element_type=jnp.float32) / student_temp
    exp_logits = jnp.exp(logits)
    denominator = lax.psum(jnp.sum(exp_logits, 1), "protos")
    grad_logits = (
        loss_scale / student_temp * (exp_logits / denominator[:, None] - target_rows)
    ).astype(jnp.bfloat16)
    partial_unit = jnp.einsum(
        "sk,dk->sd", grad_logits, w_unit_b, preferred_element_type=jnp.float32
    )
    grad_unit = lax.psum(partial_unit, "protos")
    grad_rows = (grad_unit - stu_unit * jnp.sum(stu_unit * grad_unit, 1, keepdims=True)) / u_norm
    returned = lax.all_to_all(grad_rows, "rows", split_axis=0, concat_axis=0, tiled=True)
    grad_students = returned[jnp.argsort(send_order)]
    feature_share = prototypes.shape[0] // row_devices
    first_feature = lax.axis_index("rows") * feature_share
    grad_share = lax.psum_scatter(
        jnp.einsum("sd,sk->dk", stu_unit_b, grad_logits, preferred_element_type=jnp.float32),
        "rows",
        scatter_dimension=0,
        tiled=True,
    )
    unit_share = lax.dynamic_slice_in_dim(w_unit, first_feature, feature_share, 0)
    inner = lax.psum(jnp.sum(unit_share * grad_share, 0), "rows")
    grad_protos = (grad_share - unit_share * inner[None, :]) / w_norm
    return (grad_students, grad_protos)


def solution(mesh):
    in_specs = (P("rows", None), P("rows", None), P(None, "protos"), P("rows"), P("rows"))
    out_specs = (P("rows", None), P("rows", "protos"))
    return jax.shard_map(body, mesh=mesh, in_specs=in_specs, out_specs=out_specs, check_vma=False)
```

profile of v0, /device:TPU:1, one launch (start us, length us, event | category | flops | bytes accessed | tf_op | source)
XLA Modules:
  0.0 577.3 jit_solution(10090649880890800840)
XLA Ops:
  8.0 0.0 copy-start
  8.0 3.9 sort.34
  11.9 2.0 gather_fusion.1
  13.9 0.7 all_to_all.24
  14.6 11.1 %all-to-all-start.1 = ((s32[32,8,1]{1,2,0:T(1,128)}), s32[32,8,1]{1,2,0:T(1,128)S(1)}, u32[]{:S(2)}, u32[]{:S(2)}) async-start(s32[32,8,1]{1,2,0:T(1,128)} %bitcast.2), calls=%async_computation.1 | async-start | bytes 32768 | tf_op jit(solution)/shard_map/all_to_all | solution.py:42
  25.7 0.0 copy-start.2
  25.7 3.2 fusion.2
  29.0 0.1 fusion.5
  29.1 0.1 copy-done.2
  29.2 1.3 fusion.18
  30.5 103.9 %psum.50 = f32[8192]{0:T(1024)S(1)} all-reduce(f32[8192]{0:T(1024)S(1)} %get-tuple-element.8), channel_id=1, replica_groups=mesh['rows'=32,'protos'=8] {'rows'}, use_global_device_ids=true, to_apply=%region_7.0 | all-reduce | flops 8192 | bytes 65536 | tf_op jit(solution)/shard_map/psum | solution.py:35
  134.4 0.2 multiply_reduce_fusion.2
  134.6 20.3 %psum.51 = f32[64]{0:T(128)S(1)} all-reduce(f32[64]{0:T(128)S(1)} %multiply_reduce_fusion.2), channel_id=1, replica_groups=mesh['rows'=32,'protos'=8] {'protos'}, use_global_device_ids=true, to_apply=%region_9.0 | all-reduce | flops 64 | bytes 512 | tf_op jit(solution)/shard_map/psum | solution.py:37
  154.9 0.3 multiply_reduce_fusion.1
  155.2 108.2 %psum.52 = f32[8192]{0:T(1024)S(1)} all-reduce(f32[8192]{0:T(1024)S(1)} %multiply_reduce_fusion.1), channel_id=1, replica_groups=mesh['rows'=32,'protos'=8] {'rows'}, use_global_device_ids=true, to_apply=%region_11.12 | all-reduce | flops 8192 | bytes 65536 | tf_op jit(solution)/shard_map/psum | solution.py:35
  263.4 0.2 multiply_reduce_fusion
  263.6 1.8 gather_fusion
  265.5 8.0 %all-to-all-start = ((bf16[32,8,256]{2,1,0:T(8,128)(2,1)}), bf16[32,8,256]{2,1,0:T(8,128)(2,1)S(1)}, u32[]{:S(2)}, u32[]{:S(2)}) async-start(bf16[32,8,256]{2,1,0:T(8,128)(2,1)} %bitcast), calls=%async_computation | async-start | bytes 262144 | tf_op jit(solution)/shard_map/all_to_all | solution.py:41
  273.4 0.0 all-reduce.3.cloned.1.call-start
  273.5 0.5 broadcast.97
  274.0 0.7 reduce.4
  274.7 0.1 all_to_all.26
  274.8 7.7 %all-to-all-done = bf16[32,8,256]{2,1,0:T(8,128)(2,1)S(1)} async-done(((bf16[32,8,256]{2,1,0:T(8,128)(2,1)}), bf16[32,8,256]{2,1,0:T(8,128)(2,1)S(1)}, u32[]{:S(2)}, u32[]{:S(2)}) %all-to-all-start) | async-done | bytes 131104 | tf_op jit(solution)/shard_map/all_to_all | solution.py:41
  282.5 0.1 fusion.4
  282.6 0.1 sqrt.27
  282.7 7.6 %fusion.19 = (f32[256]{0:T(256)S(1)}, f32[256,8192]{1,0:T(8,128)}) fusion(f32[8192]{0:T(1024)S(1)} %add_sqrt_fusion, bf16[256,8192]{1,0:T(8,128)(2,1)} %param.7, f32[256]{0:T(256)S(1)} %sqrt.27, bf16[32,8,256]{2,1,0:T(8,128)(2,1)S(1)} %all-to-all-done), kind=kOutput, calls=%fused_computation.50 | convolution fusion | flops 1084423936 | bytes 12748800 | tf_op jit(solution)/shard_map/dot_general | solution.py:50
  290.3 15.7 %all-reduce = (f32[64]{0:T(128)S(1)}, f32[256]{0:T(256)S(1)}) all-reduce(f32[64]{0:T(128)S(1)} %multiply_reduce_fusion, f32[256]{0:T(256)S(1)} %get-tuple-element.10), channel_id=1, replica_groups=mesh['rows'=32,'protos'=8] {'protos'}, use_global_device_ids=true, to_apply=%region_13.14 | all-reduce | flops 320 | bytes 2560 | tf_op jit(solution)/shard_map/psum | solution.py:37
  306.0 1.9 multiply_multiply_fusion
  307.9 6.2 %gather_fusion.2 = f32[256,8192]{1,0:T(8,128)} fusion(f32[64,8192]{1,0:T(8,128)S(1)} %multiply_multiply_fusion, s32[1024]{0:T(1024)S(1)} %pad_clamp_fusion.1), kind=kCustom, calls=%fused_computation.2 | custom fusion | bytes 16778240 | tf_op jit(solution)/shard_map/gather | solution.py:45
  314.1 6.7 %multiply_convert_fusion = bf16[256,8192]{1,0:T(8,128)(2,1)S(1)} fusion(f32[256,8192]{1,0:T(8,128)} %gather_fusion.2, f32[256,8192]{1,0:T(8,128)} %get-tuple-element.11, f32[256]{0:T(256)S(1)} %get-tuple-element.7), kind=kLoop, calls=%fused_computation.11 | loop fusion | flops 8388608 | bytes 20972544 | tf_op jit(solution)/shard_map/convert_element_type | solution.py:55
  320.8 2.0 copy-done.4
  322.7 2.0 fusion.12
  324.7 0.0 all-reduce.3.cloned.1.call-update
  324.8 0.0 reduce-scatter.2.cloned.1.call-start
  324.8 6.8 %fusion.7 = f32[256,8192]{1,0:T(8,128)} fusion(bf16[256,8192]{1,0:T(8,128)(2,1)} %copy-done.4, bf16[32,8,256]{2,1,0:T(8,128)(2,1)S(1)} %all-to-all-done, f32[256]{0:T(256)S(1)} %sqrt.27), kind=kOutput, calls=%fused_computation.28 | convolution fusion | flops 1073938432 | bytes 12715008 | tf_op jit(solution)/shard_map/sd,sk->dk/dot_general | solution.py:66
  331.6 0.0 reduce-scatter.2.cloned.1.call-update
  331.6 75.1 %all-reduce.3.cloned.1.call-done = f32[256,256]{1,0:T(8,128)} async-done(((f32[256,256]{1,0:T(8,128)}), f32[256,256]{1,0:T(8,128)}) %all-reduce.3.cloned.1.call-update) | async-done | bytes 262160 | tf_op jit(solution)/shard_map/psum | solution.py:59
  406.7 1.1 multiply_reduce_fusion.4
  407.8 1.8 divide_bitcast_fusion
  409.6 13.5 %all-to-all-start.2 = ((f32[32,8,256]{2,1,0:T(8,128)}), f32[32,8,256]{2,1,0:T(8,128)S(1)}, u32[]{:S(2)}, u32[]{:S(2)}) async-start(f32[32,8,256]{2,1,0:T(8,128)} %divide_bitcast_fusion), calls=%async_computation.2 | async-start | bytes 524288 | tf_op jit(solution)/shard_map/all_to_all | solution.py:61
  423.1 6.5 %convert_divide_fusion = f32[256,8192]{1,0:T(8,128)} fusion(bf16[256,8192]{1,0:T(8,128)(2,1)} %param.7, f32[8192]{0:T(1024)S(1)} %add_sqrt_fusion), kind=kLoop, calls=%fused_computation.6 | loop fusion | flops 4194304 | bytes 12615680 | tf_op jit(solution)/shard_map/div | solution.py:23
  429.6 3.2 sort.35
  432.8 3.1 all-to-all-done.2
  435.9 1.7 gather_fusion.3
  437.6 24.7 %reduce-scatter.2.cloned.1.call-done = f32[8,8192]{1,0:T(8,128)} async-done(((f32[256,8192]{1,0:T(8,128)}), f32[8,8192]{1,0:T(8,128)}) %reduce-scatter.2.cloned.1.call-update) | async-done | bytes 262160 | tf_op jit(solution)/shard_map/reduce_scatter | solution.py:65
  462.3 1.1 multiply_reduce_fusion.3
  463.4 104.7 %psum.55 = f32[8192]{0:T(1024)S(1)} all-reduce(f32[8192]{0:T(1024)S(1)} %multiply_reduce_fusion.3), channel_id=1, replica_groups=mesh['rows'=32,'protos'=8] {'rows'}, use_global_device_ids=true, to_apply=%region_19.20 | all-reduce | flops 8192 | bytes 65536 | tf_op jit(solution)/shard_map/psum | solution.py:72
  568.1 1.8 subtract_divide_fusion
  (24 shorter events, 0.1 us)
Async XLA Ops:
  8.0 255.6 %copy-start = (bf16[256,256]{1,0:T(8,128)(2,1)S(1)}, bf16[256,256]{1,0:T(8,128)(2,1)}, u32[]{:S(2)}) copy-start(bf16[256,256]{1,0:T(8,128)(2,1)} %param.6) | copy-start | bytes 393220
  8.0 21.0 %copy-start.5 = (bf16[64,256]{1,0:T(8,128)(2,1)S(1)}, bf16[64,256]{1,0:T(8,128)(2,1)}, u32[]{:S(2)}) copy-start(bf16[64,256]{1,0:T(8,128)(2,1)} %param.5) | copy-start | bytes 98308
  14.6 250.9 %all-to-all-start.1 = ((s32[32,8,1]{1,2,0:T(1,128)}), s32[32,8,1]{1,2,0:T(1,128)S(1)}, u32[]{:S(2)}, u32[]{:S(2)}) async-start(s32[32,8,1]{1,2,0:T(1,128)} %bitcast.2), calls=%async_computation.1 | async-start | bytes 32768 | tf_op jit(solution)/shard_map/all_to_all | solution.py:42
  25.7 3.5 copy-start.2
  30.5 259.8 %copy-start.1 = (f32[64,8192]{1,0:T(8,128)}, f32[64,8192]{1,0:T(8,128)S(1)}, u32[]{:S(2)}) copy-start(f32[64,8192]{1,0:T(8,128)S(1)} %get-tuple-element.9) | copy-start | bytes 6291460
  265.5 17.0 %all-to-all-start = ((bf16[32,8,256]{2,1,0:T(8,128)(2,1)}), bf16[32,8,256]{2,1,0:T(8,128)(2,1)S(1)}, u32[]{:S(2)}, u32[]{:S(2)}) async-start(bf16[32,8,256]{2,1,0:T(8,128)(2,1)} %bitcast), calls=%async_computation | async-start | bytes 262144 | tf_op jit(solution)/shard_map/all_to_all | solution.py:41
  273.4 133.3 %all-reduce.3.cloned.1.call-start = ((), (), s32[]{:S(2)}) async-start(), calls=%async_computation.4 | async-start | bytes 524288 | tf_op jit(solution)/shard_map/psum | solution.py:59
  314.1 8.7 %copy-start.3 = (bf16[256,8192]{1,0:T(8,128)(2,1)S(1)}, bf16[256,8192]{1,0:T(8,128)(2,1)}, u32[]{:S(2)}) copy-start(bf16[256,8192]{1,0:T(8,128)(2,1)} %param.7) | copy-start | bytes 12582916
  320.8 2.0 copy-start.4
  324.8 137.5 %reduce-scatter.2.cloned.1.call-start = ((), (), s32[]{:S(2)}) async-start(), calls=%async_computation.5 | async-start | bytes 8650752 | tf_op jit(solution)/shard_map/reduce_scatter | solution.py:65
  409.6 26.3 %all-to-all-start.2 = ((f32[32,8,256]{2,1,0:T(8,128)}), f32[32,8,256]{2,1,0:T(8,128)S(1)}, u32[]{:S(2)}, u32[]{:S(2)}) async-start(f32[32,8,256]{2,1,0:T(8,128)} %divide_bitcast_fusion), calls=%async_computation.2 | async-start | bytes 524288 | tf_op jit(solution)/shard_map/all_to_all | solution.py:61
Sparse Core Ops, SparseCore 0:
  324.9 81.7 all-reduce.2
Sparse Core Ops, SparseCore 1:
  331.7 130.5 reduce-scatter.1
where the time goes:
time: 581 us; the launch traced here: 577 us
  blocking collectives  353 us (61%)
  waiting for transfers between devices  111 us (19%)
  other arithmetic  32.9 us (6%)
  starting transfers between devices  32.7 us (6%)
  matrix products  17.7 us (3%)
  between operations  15.7 us (3%)
  local copies, waits for them, and re-layouts  15.1 us (3%)
    psum x2, blocking collectives, body(): colsum = lax.psum(jnp.sum(exp_scores * row_factor[:, None], 0), 'rows')  212 us
    psum x1, blocking collectives, body(): inner = lax.psum(jnp.sum(unit_share * grad_share, 0), 'rows')  105 us
    psum x1, waiting for transfers between devices, body(): grad_unit = lax.psum(partial_unit, 'protos')  75.1 us
    psum x2, blocking collectives, body(): rowsum = lax.psum(jnp.sum(exp_scores * col_factor[None, :], 1), 'protos')  35.9 us
    reduce_scatter x1, waiting for transfers between devices, body(): lax.psum_scatter(jnp.einsum('sd,sk->dk', stu_unit_b, grad_logits, preferr...  24.7 us
    all_to_all x1, starting transfers between devices, body(): lax.all_to_all(grad_rows, 'rows', split_axis=0, concat_axis=0, tiled=True)  13.5 us
  transfers between devices with their start and end apart: 5, of which 4 were waited for; matrix products, arithmetic and copies ran while one was open for 5% of the time, Pallas kernels for 0%

commit v1 on v0

v1 whole, which is shorter than its diff:
```python
import functools

import jax
import jax.numpy as jnp
from jax import lax
from jax.experimental import pallas as pl
from jax.experimental.pallas import tpu as pltpu
from jax.sharding import PartitionSpec as P

F32 = jnp.float32
BF = jnp.bfloat16
MESH = pl.DeviceIdType.MESH

epsilon = 1e-06
teacher_temp = 0.07
student_temp = 0.1
loss_scale = 16.0

NT = (((1,), (1,)), ((), ()))
TN = (((0,), (0,)), ((), ()))


def dot(a, b):
    return jnp.dot(a, b, preferred_element_type=F32)


def dotg(a, b, dims):
    return lax.dot_general(a, b, dims, preferred_element_type=F32)


def iota(shape, dim):
    return lax.broadcasted_iota(jnp.int32, shape, dim)


def to_col(row, n):
    eye = iota((n, n), 0) == iota((n, n), 1)
    return jnp.sum(jnp.where(eye, jnp.broadcast_to(row, (n, n)), 0.0), 1, keepdims=True)


def to_row(col, n):
    eye = iota((n, n), 0) == iota((n, n), 1)
    return jnp.sum(jnp.where(eye, jnp.broadcast_to(col, (n, n)), 0.0), 0, keepdims=True)


def lane_fold(x):
    total = x[:, 0:128]
    for k in range(1, x.shape[1] // 128):
        total = total + x[:, k * 128:(k + 1) * 128]
    return total


class Refs:
    pass


def plan(NR, NP, T, S, D, CL):
    Z = NR // 4
    CZ = CL // Z
    B = S // NR
    FB = D // NR
    RB = S // NP
    shapes = dict(
        tq=((Z, T, D), BF),
        sb=((S, D), BF),
        pt=((S, S), F32),
        ssort=((4, S // 4, D), BF),
        msort=((4, 1, 128), F32),
        stu=((Z, 4, S // 4, D), BF),
        meta=((Z, 4, 1, 128), F32),
        w_b=((D, CL), BF),
        wzf=((D, CZ), F32),
        wz=((D, CZ), BF),
        nz=((1, CZ), F32),
        a2=((S, CL), F32),
        t2=((S, CL), F32),
        dsrc=((1, S), F32),
        drecv=((NP - 1, 1, S), F32),
        dq=((4, 1, 128), F32),
        dm=((Z, 4, 1, 128), F32),
        e1=((Z // 2, 128, CZ), F32),
        esp=((Z // 2, 256, CZ), BF),
        cs=((2, 1, CZ), F32),
        csr=((2, 3, 1, CZ), F32),
        rs=((2, 1, Z * T), F32),
        rsr=((2, Z - 1, 1, Z * T), F32),
        rp=((2, 1, Z * T), F32),
        rpr=((2, NP - 1, 1, Z * T), F32),
        tss=((4, S // 4, D), BF),
        ts=((4, S // 4, D), BF),
        tsh=((S, D), BF),
        va=((Z, 1, CZ), F32),
        a1=((Z // 2, 512, CZ), F32),
        t1=((Z // 2, 512, CZ), F32),
        st=((Z // 2, D, 512), BF),
        idxc=((Z // 2, 512, 128), F32),
        uss=((4, 1, 128), F32),
        us=((4, 1, 128), F32),
        gu=((NP, RB, D), F32),
        gur=((NP - 1, RB, D), F32),
        gsr=((NP, RB, D), F32),
        gw=((2, 2, Z, FB, CZ), F32),
        gwr=((2, Z, FB, CZ), F32),
        gy=((Z, FB, CZ), F32),
        gyr=((Z, FB, CZ), F32),
        ins=((1, CZ), F32),
        inr=((3, 1, CZ), F32),
        go=((Z, FB, CZ), F32),
        gpr=((Z, FB, CZ), F32),
    )
    return shapes


NSEM = 128


def kernel(dims, tea_ref, stu_ref, proto_ref, lay_r, lay_c, pair_c, gs_out, gp_out, *scratch):
    NR, NP, T, S, D, CL = dims
    Z = NR // 4
    CZ = CL // Z
    B = S // NR
    RPR = 2 * B
    FB = D // NR
    RB = S // NP
    PAIRS = Z // 2
    TEACHERS = T * NR
    PROTOS = CL * NP
    GS = loss_scale / student_temp
    names = list(plan(*dims))
    m = Refs()
    for name, ref in zip(names, scratch):
        setattr(m, name, ref)
    send_sem, recv_sem = scratch[len(names):]

    r = lax.axis_index("rows")
    p = lax.axis_index("protos")
    core = lax.rem(r, 2)
    z = lax.rem(r // 2, Z)
    yl = r // (2 * Z)
    qd = yl * 2 + core

    def row(y_, z_, c_):
        return (y_ * Z + z_) * 2 + c_

    zs = [lax.rem(z + d, Z) for d in range(1, Z)]
    zdev = [(row(yl, z2, core), p) for z2 in zs]
    ps = [lax.rem(p + d, NP) for d in range(1, NP)]
    pdev = [(r, p2) for p2 in ps]
    qs, qdev = [], []
    for d in (1, 2, 3):
        c2 = 1 - core if d & 1 else core
        y2 = 1 - yl if d & 2 else yl
        qs.append(y2 * 2 + c2)
        qdev.append((row(y2, z, c2), p))

    sent = []
    counter = [0]

    def start(copies):
        handles = []
        for src, dst, dev in copies:
            i = counter[0]
            counter[0] += 1
            h = pltpu.make_async_remote_copy(
                src_ref=src, dst_ref=dst, send_sem=send_sem.at[i], recv_sem=recv_sem.at[i],
                device_id=dev, device_id_type=MESH)
            h.start()
            handles.append(h)
            sent.append(h)
        return handles

    def arrive(handles):
        for h in handles:
            h.wait_recv()

    bar = pltpu.get_barrier_semaphore()
    everyone = zdev + pdev + qdev
    for dev in everyone:
        pl.semaphore_signal(bar, inc=1, device_id=dev, device_id_type=MESH)

    te = tea_ref[...].astype(F32)
    m.tq[z] = (te / jnp.sqrt(jnp.sum(te * te, 1, keepdims=True) + epsilon)).astype(BF)
    st = stu_ref[...].astype(F32)
    m.sb[...] = (st / jnp.sqrt(jnp.sum(st * st, 1, keepdims=True) + epsilon)).astype(BF)
    lc = lay_c[...]
    lr = lay_r[...]
    same = (lc == lr) & (iota((S, S), 1) < iota((S, S), 0))
    rank = jnp.sum(jnp.where(same, 1.0, 0.0), 1, keepdims=True)
    zt = lax.rem(lc // 2, Z)
    key = ((lc // (2 * Z)) * 2 + lax.rem(lc, 2)) * Z + zt
    pos = (key * B).astype(F32) + rank
    m.pt[...] = jnp.where(iota((S, S), 1).astype(F32) == pos, 1.0, 0.0)
    idx = (lax.rem(zt, 2) * T + pair_c[...]).astype(F32)
    m.ssort[...] = dotg(m.pt[...].astype(BF), m.sb[...], TN).astype(BF).reshape(4, S // 4, D)
    isort = jnp.sum(m.pt[...] * idx, 0, keepdims=True)
    spare = jnp.zeros((1, 64), F32)
    for q in range(4):
        m.msort[q] = jnp.concatenate([isort[:, q * 64:(q + 1) * 64], spare], 1)
    m.stu[z, qd] = m.ssort[qd]
    m.meta[z, qd] = m.msort[qd]

    pl.semaphore_wait(bar, len(everyone))

    c_tea = start([(m.tq.at[z], m.tq.at[z], dev) for dev in zdev])
    c_meta = start([(m.msort.at[q], m.meta.at[z, qd], dev) for q, dev in zip(qs, qdev)])
    c_stu = start([(m.ssort.at[q], m.stu.at[z, qd], dev) for q, dev in zip(qs, qdev)])

    @pl.loop(0, CZ // 256)
    def _(i):
        c = pl.multiple_of(i * 256, 256)
        w = proto_ref[:, pl.ds(pl.multiple_of(z * CZ + c, 256), 256)].astype(F32)
        n = jnp.sqrt(jnp.sum(w * w, 0, keepdims=True) + epsilon)
        u = w / n
        m.nz[:, pl.ds(c, 256)] = n
        m.wzf[:, pl.ds(c, 256)] = u
        m.wz[:, pl.ds(c, 256)] = u.astype(BF)

    @pl.loop(0, CL // 256)
    def _(i):
        c = pl.multiple_of(i * 256, 256)
        w = proto_ref[:, pl.ds(c, 256)].astype(F32)
        n = jnp.sqrt(jnp.sum(w * w, 0, keepdims=True) + epsilon)
        m.w_b[:, pl.ds(c, 256)] = (w / n).astype(BF)

    arrive(c_meta)
    arrive(c_stu)

    zr, zl = lax.rem(z + 1, Z), lax.rem(z + Z - 1, Z)
    right, left = (row(yl, zr, core), p), (row(yl, zl, core), p)
    ring = []

    def ring_step(s):
        if ring:
            arrive(ring[-1])
        a = lax.rem(z + Z - (s - 1), Z)
        b = lax.rem(z + (s - 1), Z)
        if s < Z // 2:
            ring.append(start([(m.stu.at[a], m.stu.at[a], right), (m.stu.at[b], m.stu.at[b], left)]))
        else:
            ring.append(start([
                (m.stu.at[a, pl.ds(0, 2)], m.stu.at[a, pl.ds(0, 2)], right),
                (m.stu.at[b, pl.ds(2, 2)], m.stu.at[b, pl.ds(2, 2)], left)]))

    steps = list(range(1, Z // 2 + 1))

    def next_ring():
        if steps:
            ring_step(steps.pop(0))

    next_ring()
    c_metaz = start([(m.meta.at[z], m.meta.at[z], dev) for dev in zdev])

    m.drow = None

    def a2_step(i, acc):
        c = pl.multiple_of(i * 512, 512)
        a = jnp.exp(dot(m.sb[...], m.w_b[:, pl.ds(c, 512)]) * (1.0 / student_temp))
        m.a2[:, pl.ds(c, 512)] = a
        return acc + lane_fold(a)

    acc = lax.fori_loop(0, CL // 512, a2_step, jnp.zeros((S, 128), F32))
    m.dsrc[...] = to_row(jnp.sum(acc, 1, keepdims=True), S)
    c_den = start([(m.dsrc, m.drecv.at[d], dev) for d, dev in enumerate(pdev)])

    arrive(c_tea)
    m.cs[0] = jnp.zeros((1, CZ), F32)

    @pl.loop(0, PAIRS)
    def _(k):
        tk = m.tq[pl.ds(k * 2, 2)].reshape(2 * T, D)
        for c in range(0, CZ, 512):
            e = jnp.exp(dot(tk, m.wz[:, c:c + 512]) * (1.0 / teacher_temp))
            m.e1[k, :, c:c + 512] = e
            hi = e.astype(BF)
            m.esp[k, 0:128, c:c + 512] = hi
            m.esp[k, 128:256, c:c + 512] = (e - hi.astype(F32)).astype(BF)
            m.cs[0, :, c:c + 512] += jnp.sum(e, 0, keepdims=True)

    c_cs = start([(m.cs.at[0], m.csr.at[0, d], dev) for d, dev in enumerate(qdev)])

    for k in range(PAIRS):
        rows = jnp.broadcast_to(m.meta[z], (4, RPR, 128)).reshape(4 * RPR, 128)
        mine = iota((4, RPR, 128), 2) == iota((4, RPR, 128), 1) + k * RPR
        col = jnp.sum(jnp.where(mine.reshape(4 * RPR, 128), rows, 0.0), 1, keepdims=True)
        hot = jnp.where(iota((4 * RPR, 128), 1).astype(F32) == col, 1.0, 0.0).astype(BF)
        got = dot(hot, m.tq[2 * k:2 * k + 2].reshape(2 * T, D)).astype(BF)
        m.tss[:, k * RPR:(k + 1) * RPR, :] = got.reshape(4, RPR, D)
    m.ts[qd] = m.tss[qd]
    c_ts = start([(m.tss.at[q], m.ts.at[qd], dev) for q, dev in zip(qs, qdev)])

    next_ring()

    def col_factor(it, c_cs):
        arrive(c_cs)
        return 1.0 / (PROTOS * (m.cs[it] + m.csr[it, 0] + m.csr[it, 1] + m.csr[it, 2]))

    def send_rowsum(it, v):
        for k in range(PAIRS):
            part = lane_fold(m.e1[k] * v)
            m.rs[it, :, k * 128:(k + 1) * 128] = to_row(jnp.sum(part, 1, keepdims=True), 128)
        return start([(m.rs.at[it], m.rsr.at[it, d], dev) for d, dev in enumerate(zdev)])

    def send_rowsum_protos(it, c_rs):
        arrive(c_rs)
        total = m.rs[it]
        for d in range(Z - 1):
            total = total + m.rsr[it, d]
        m.rp[it] = total
        return start([(m.rp.at[it], m.rpr.at[it, d], dev) for d, dev in enumerate(pdev)])

    def row_factor(it, c_rp):
        arrive(c_rp)
        total = m.rp[it]
        for d in range(NP - 1):
            total = total + m.rpr[it, d]
        return 1.0 / (TEACHERS * total)

    v1 = col_factor(0, c_cs)
    c_rs = send_rowsum(0, v1)

    arrive(c_den)
    den = m.dsrc[...]
    for d in range(NP - 1):
        den = den + m.drecv[d]
    sc2 = GS / to_col(den, S)
    scs = jnp.sum(m.pt[...] * sc2, 0, keepdims=True)
    for q in range(4):
        m.dq[q] = jnp.concatenate([scs[:, q * 64:(q + 1) * 64], spare], 1)
    m.dm[z, qd] = m.dq[qd]
    c_dq = start([(m.dq.at[q], m.dm.at[z, qd], dev) for q, dev in zip(qs, qdev)])
    arrive(c_ts)
    m.tsh[...] = dot(m.pt[...].astype(BF), m.ts[...].reshape(S, D)).astype(BF)
    arrive(c_dq)
    c_dz = start([(m.dm.at[z], m.dm.at[z], dev) for dev in zdev])

    c_rp = send_rowsum_protos(0, c_rs)
    next_ring()

    def t2_range(lo, hi):
        @pl.loop(lo, hi)
        def _(i):
            c = pl.multiple_of(i * 512, 512)
            m.t2[:, pl.ds(c, 512)] = jnp.exp(dot(m.tsh[...], m.w_b[:, pl.ds(c, 512)]) * (1.0 / teacher_temp))

    t2_range(0, CL // 512)

    u1 = row_factor(0, c_rp)
    part = jnp.zeros((1, CZ), F32)
    for k in range(PAIRS):
        uc = to_col(u1[:, k * 128:(k + 1) * 128], 128)
        part = part + jnp.sum(m.e1[k] * uc, 0, keepdims=True)
    m.cs[1] = part
    c_cs = start([(m.cs.at[1], m.csr.at[1, d], dev) for d, dev in enumerate(qdev)])
    next_ring()
    v2 = col_factor(1, c_cs)
    c_rs = send_rowsum(1, v2)
    m.va[z] = v2
    c_va = start([(m.va.at[z], m.va.at[z], dev) for dev in zdev])

    while steps:
        next_ring()
    arrive(ring[-1])
    arrive(c_metaz)
    arrive(c_dz)

    def block_col(ref, k):
        rows = jnp.broadcast_to(ref[...].reshape(NR, 1, 128), (NR, RPR, 128)).reshape(512, 128)
        mine = (iota((NR, RPR, 128), 2) == iota((NR, RPR, 128), 1) + k * RPR).reshape(512, 128)
        return jnp.sum(jnp.where(mine, rows, 0.0), 1, keepdims=True)

    def layout1(k):
        sk = m.stu[:, :, pl.ds(pl.multiple_of(k * RPR, RPR), RPR), :].reshape(512, D)
        m.st[k] = sk.T
        ic = block_col(m.meta, k)
        m.idxc[k] = jnp.broadcast_to(ic, (512, 128))
        sc = block_col(m.dm, k)
        hot = jnp.where(iota((512, 128), 1).astype(F32) == ic, 1.0, 0.0).astype(BF)
        hot = jnp.concatenate([hot, hot], 1)

        @pl.loop(0, CZ // 256)
        def _(i):
            c = pl.multiple_of(i * 256, 256)
            m.a1[k, :, pl.ds(c, 256)] = jnp.exp(dot(sk, m.wz[:, pl.ds(c, 256)]) * (1.0 / student_temp)) * sc
            m.t1[k, :, pl.ds(c, 256)] = dot(hot, m.esp[k, :, pl.ds(c, 256)])

    for k in range(PAIRS // 2):
        layout1(k)
    c_rp = send_rowsum_protos(1, c_rs)
    for k in range(PAIRS // 2, PAIRS):
        layout1(k)
    arrive(c_va)
    u2 = row_factor(1, c_rp) * (GS * TEACHERS)

    sel = [jnp.zeros((1, 128), F32)] * 4
    for k in range(PAIRS):
        uc = to_col(u2[:, k * 128:(k + 1) * 128], 128)
        lane = iota((128, 128), 1)
        span = (lane >= k * RPR) & (lane < (k + 1) * RPR)
        for q in range(4):
            hit = (iota((128, 128), 0).astype(F32) == m.meta[z, q]) & span
            sel[q] = sel[q] + jnp.sum(jnp.where(hit, uc, 0.0), 0, keepdims=True)
    for q in range(4):
        m.uss[q] = sel[q]
    m.us[qd] = m.uss[qd]
    c_us = start([(m.uss.at[q], m.us.at[qd], dev) for q, dev in zip(qs, qdev)])
    arrive(c_us)

    urow = jnp.concatenate([m.us[q][:, 0:64] for q in range(4)], 1)
    ucol = jnp.sum(m.pt[...] * urow, 1, keepdims=True)
    sc2 = GS / to_col(den, S)

    def g2_step(i, acc):
        c = pl.multiple_of(i * 512, 512)
        zi = i // (CZ // 512)
        vv = m.va[zi, :, pl.ds(pl.multiple_of(c - zi * CZ, 512), 512)]
        g = (m.a2[:, pl.ds(c, 512)] * sc2 - m.t2[:, pl.ds(c, 512)] * vv * ucol).astype(BF)
        return acc + dotg(g, m.w_b[:, pl.ds(c, 512)], NT)

    gsum = lax.fori_loop(0, CL // 512, g2_step, jnp.zeros((S, D), F32))
    m.gu[...] = gsum.reshape(NP, RB, D)
    c_gu = start([(m.gu.at[p2], m.gur.at[d], dev) for d, (p2, dev) in enumerate(zip(ps, pdev))])

    ucs = []
    for k in range(PAIRS):
        hit = iota((512, 128), 1).astype(F32) == m.idxc[k]
        ucs.append(jnp.sum(jnp.where(hit, jnp.broadcast_to(u2[:, k * 128:(k + 1) * 128], (512, 128)), 0.0), 1, keepdims=True))

    for c in range(0, CZ, 256):
        vv = m.va[z, :, c:c + 256]
        total = None
        for k in range(PAIRS):
            g = (m.a1[k, :, c:c + 256] - m.t1[k, :, c:c + 256] * vv * ucs[k]).astype(BF)
            one = dot(m.st[k], g)
            total = one if total is None else total + one
        m.ins[:, c:c + 256] = jnp.sum(m.wzf[:, c:c + 256] * total, 0, keepdims=True)
        for y_ in range(2):
            for z_ in range(Z):
                for c_ in range(2):
                    f = ((y_ * Z + z_) * 2 + c_) * FB
                    m.gw[c_, y_, z_, :, c:c + 256] = total[f:f + FB, :]

    c_gw = start([(m.gw.at[1 - core], m.gwr, qdev[0])])
    c_in = start([(m.ins, m.inr.at[d], dev) for d, dev in enumerate(qdev)])

    arrive(c_gu)
    gsum = m.gu[p]
    for d in range(NP - 1):
        gsum = gsum + m.gur[d]
    su = stu_ref[pl.ds(pl.multiple_of(p * RB, RB), RB), :].astype(F32)
    un = jnp.sqrt(jnp.sum(su * su, 1, keepdims=True) + epsilon)
    su = su / un
    m.gsr[p] = (gsum - su * jnp.sum(su * gsum, 1, keepdims=True)) / un
    c_gs = start([(m.gsr.at[p], m.gsr.at[p], dev) for dev in pdev])

    arrive(c_gw)
    m.gy[...] = m.gw[core, 1 - yl] + m.gwr[1 - yl]
    c_gy = start([(m.gy, m.gyr, qdev[1])])
    mine = m.gw[core, yl] + m.gwr[yl]
    arrive(c_in)
    inner = m.ins[...] + m.inr[0] + m.inr[1] + m.inr[2]
    arrive(c_gy)
    inv = 1.0 / m.nz[...]
    for z_ in range(Z):
        f = pl.multiple_of(row(yl, z_, core) * FB, FB)
        m.go[z_] = (mine[z_] + m.gyr[z_] - m.wzf[pl.ds(f, FB), :] * inner) * inv
    m.gpr[z] = m.go[z]
    c_gp = start([(m.go.at[z2], m.gpr.at[z], dev) for z2, dev in zip(zs, zdev)])
    arrive(c_gs)
    gs_out[...] = m.gsr[...].reshape(S, D)
    arrive(c_gp)
    for z_ in range(Z):
        gp_out[:, z_ * CZ:(z_ + 1) * CZ] = m.gpr[z_]
    for h in sent:
        h.wait_send()


def body(teacher, students, prototypes, pairing, layout):
    NR = lax.axis_size("rows")
    NP = lax.axis_size("protos")
    T, D = teacher.shape
    S = students.shape[0]
    CL = prototypes.shape[1]
    dims = (NR, NP, T, S, D, CL)
    vmem = pl.BlockSpec(memory_space=pltpu.VMEM)
    scratch = [pltpu.VMEM(shape, dtype) for shape, dtype in plan(*dims).values()]
    scratch += [pltpu.SemaphoreType.DMA((NSEM,)), pltpu.SemaphoreType.DMA((NSEM,))]
    return pl.pallas_call(
        functools.partial(kernel, dims),
        out_shape=(
            jax.ShapeDtypeStruct((S, D), F32),
            jax.ShapeDtypeStruct((D // NR, CL), F32),
        ),
        in_specs=[vmem] * 6,
        out_specs=(vmem, vmem),
        scratch_shapes=scratch,
        compiler_params=pltpu.CompilerParams(
            collective_id=0, has_side_effects=True, vmem_limit_bytes=62 * 1024 * 1024
        ),
        name="distill",
    )(teacher, students, prototypes, layout.reshape(1, S), layout.reshape(S, 1), pairing.reshape(S, 1))


def solution(mesh):
    in_specs = (P("rows", None), P("rows", None), P(None, "protos"), P("rows"), P("rows"))
    out_specs = (P("rows", None), P("rows", "protos"))
    return jax.shard_map(body, mesh=mesh, in_specs=in_specs, out_specs=out_specs, check_vma=False)
```

time: 581 us -> 88 us (0.15)
  blocking collectives: 353 us -> 0 us
  waiting for transfers between devices: 111 us -> 0 us
  Pallas kernels: 0 us -> 80.4 us
  other arithmetic: 32.9 us -> 0 us
  starting transfers between devices: 32.7 us -> 0 us
  matrix products: 17.7 us -> 0 us
  between operations: 15.7 us -> 0.64 us
  local copies, waits for them, and re-layouts: 15.1 us -> 6.28 us
    psum x5 -> x0, blocking collectives: 353 us -> none  [the longest x2 212 us: body(): colsum = lax.psum(jnp.sum(exp_scores * row_factor[:, None], 0), 'rows')]
    pallas_call x0 -> x1, Pallas kernels: none -> 80.4 us  [body(): pl.pallas_call(functools.partial(kernel, dims), out_shape=(jax.ShapeDtype...]
    psum x1 -> x0, waiting for transfers between devices: 75.1 us -> none  [body(): grad_unit = lax.psum(partial_unit, 'protos')]
    all_to_all x3 -> x0, starting transfers between devices: 32.6 us -> none  [the longest x1 13.5 us: body(): lax.all_to_all(grad_rows, 'rows', split_axis=0, concat_axis=0, tiled=True)]
    reduce_scatter x1 -> x0, waiting for transfers between devices: 24.7 us -> none  [body(): lax.psum_scatter(jnp.einsum('sd,sk->dk', stu_unit_b, grad_logits, preferr...]
    dot_general x4 -> x0, matrix products: 17.7 us -> none  [the longest x1 7.62 us: body(): jnp.dot(stu_unit_b, w_unit_b, preferred_element_type=jnp.float32)]
    gather x4 -> x0, local copies, waits for them, and re-layouts: 11.6 us -> none  [the longest x1 6.19 us: body(): target_rows = balanced[moved_pairs]]
    all_to_all x3 -> x0, waiting for transfers between devices: 10.8 us -> none  [the longest x1 7.71 us: body(): lax.all_to_all(students[send_order], 'rows', split_axis=0, concat_axis=0,...]
  transfers between devices with their start and end apart: 5 -> 0, of which waited for: 4 -> 0; matrix products, arithmetic and copies ran while one was open for 5% -> 0% of each run, Pallas kernels for 0% -> 0%
where the time goes in v1:
time: 88 us; the launch traced here: 87.3 us
  Pallas kernels  80.4 us (91%)
  local copies, waits for them, and re-layouts  6.28 us (7%)
    pallas_call x1, Pallas kernels, body(): pl.pallas_call(functools.partial(kernel, dims), out_shape=(jax.ShapeDtype...  80.4 us
    unnamed x2, local copies, waits for them, and re-layouts  3.34 us

profile of v1, /device:TPU:1, one launch (start us, length us, event | category | flops | bytes accessed | tf_op | source)
XLA Modules:
  0.0 87.3 jit_solution(12556577400530206084)
XLA Ops:
  0.6 1.5 %copy.8.pair_c = s32[256,1]{1,0:T(8,128)} copy(s32[256,1]{0,1:T(1,128)} %bitcast.5) | data formatting | bytes 2048 | tf_op jit(solution)/shard_map/reshape | solution.py:499
  2.1 1.5 %copy.7.lay_c = s32[256,1]{1,0:T(8,128)} copy(s32[256,1]{0,1:T(1,128)} %bitcast.3) | data formatting | bytes 2048 | tf_op jit(solution)/shard_map/reshape | solution.py:499
  3.6 80.4 %distill.1 = (f32[256,256]{1,0:T(8,128)}, f32[8,8192]{1,0:T(8,128)}) custom-call(bf16[64,256]{1,0:T(8,128)(2,1)} %tea_ref.1, bf16[256,256]{1,0:T(8,128)(2,1)} %stu_ref.1, bf16[256,8192]{1,0:T(8,128)(2,1)} %proto_ref.1, s32[1,256]{1,0:T(1,128)} %bitcast.4, s32[256,1]{1,0:T(8,128)} %copy.7.lay_c, s32[256,1]{1,0:T(8,128)} %copy.8.pair_c), custom_call_target="tpu_custom_call" | custom-call | tf_op jit(solution)/shard_map/distill/pallas_call | solution.py:486
  84.0 1.7 %copy.11 = f32[256,256]{1,0:T(8,128)} copy(f32[256,256]{1,0:T(8,128)} %get-tuple-element.4) | data formatting | bytes 524288
  85.7 1.7 %copy.12 = f32[8,8192]{1,0:T(8,128)} copy(f32[8,8192]{1,0:T(8,128)} %get-tuple-element.5) | data formatting | bytes 524288

commit v2 on v1

v2 whole, which is shorter than its diff:
```python
import functools

import jax
import jax.numpy as jnp
from jax import lax
from jax.experimental import pallas as pl
from jax.experimental.pallas import tpu as pltpu
from jax.sharding import PartitionSpec as P

F32 = jnp.float32
BF = jnp.bfloat16
MESH = pl.DeviceIdType.MESH

epsilon = 1e-06
teacher_temp = 0.07
student_temp = 0.1
loss_scale = 16.0

NT = (((1,), (1,)), ((), ()))
TN = (((0,), (0,)), ((), ()))


def dot(a, b):
    return jnp.dot(a, b, preferred_element_type=F32)


def dotg(a, b, dims):
    return lax.dot_general(a, b, dims, preferred_element_type=F32)


def iota(shape, dim):
    return lax.broadcasted_iota(jnp.int32, shape, dim)


def to_col(row, n):
    eye = iota((n, n), 0) == iota((n, n), 1)
    return jnp.sum(jnp.where(eye, jnp.broadcast_to(row, (n, n)), 0.0), 1, keepdims=True)


def to_row(col, n):
    eye = iota((n, n), 0) == iota((n, n), 1)
    return jnp.sum(jnp.where(eye, jnp.broadcast_to(col, (n, n)), 0.0), 0, keepdims=True)


def lane_fold(x):
    total = x[:, 0:128]
    for k in range(1, x.shape[1] // 128):
        total = total + x[:, k * 128:(k + 1) * 128]
    return total


class Refs:
    pass


def plan(NR, NP, T, S, D, CL):
    Z = NR // 4
    CZ = CL // Z
    CQ = CL // 4
    FB = D // NR
    RB = S // NP
    PLANE = 4 * NP - 1
    shapes = dict(
        pr=((D, CL), BF),
        tp=((4, T, D), BF),
        tq=((Z, T, D), BF),
        sb=((S, D), BF),
        pt=((S, S), F32),
        ssort=((4, S // 4, D), BF),
        msort=((4, 1, 128), F32),
        stu=((Z, 4, S // 4, D), BF),
        meta=((Z, 4, 1, 128), F32),
        w_b=((D, CL), BF),
        wzf=((D, CZ), F32),
        wz=((D, CZ), BF),
        nz=((1, CZ), F32),
        a2=((S, CL), F32),
        t2=((S, CL), F32),
        dsrc=((1, S), F32),
        drecv=((NP - 1, 1, S), F32),
        dq=((4, 1, 128), F32),
        dm=((Z, 4, 1, 128), F32),
        e8=((4 * T, CQ), F32),
        esp=((Z // 2, 256, CZ), BF),
        cs=((2, 1, CQ), F32),
        csr=((2, Z - 1, 1, CQ), F32),
        rs=((2, 1, 4 * T), F32),
        rsr=((2, PLANE, 1, 4 * T), F32),
        ua=((Z, 1, 4 * T), F32),
        tss=((4, S // 4, D), BF),
        ts=((4, S // 4, D), BF),
        tsh=((S, D), BF),
        va=((4, 1, CQ), F32),
        a1=((Z // 2, 512, CZ), F32),
        t1=((Z // 2, 512, CZ), F32),
        st=((Z // 2, D, 512), BF),
        idxc=((Z // 2, 512, 128), F32),
        gu=((NP, RB, D), F32),
        gur=((NP - 1, RB, D), F32),
        gsr=((NP, RB, D), F32),
        gw=((2, 2, 2, Z, FB, CZ // 2), F32),
        gwr=((2, 2, Z, FB, CZ // 2), F32),
        gy=((2, Z, FB, CZ // 2), F32),
        gyr=((2, Z, FB, CZ // 2), F32),
        ins=((2, 1, CZ // 2), F32),
        inr=((2, 3, 1, CZ // 2), F32),
        go=((2, Z, FB, CZ // 2), F32),
        gpr=((2, Z, FB, CZ // 2), F32),
    )
    return shapes


NSEM = 192


def kernel(dims, tea_ref, stu_ref, proto_ref, lay_ref, pair_ref, gs_out, gp_out, *scratch):
    NR, NP, T, S, D, CL = dims
    Z = NR // 4
    CZ = CL // Z
    CQ = CL // 4
    CH = CZ // 2
    B = S // NR
    RPR = 2 * B
    FB = D // NR
    RB = S // NP
    PAIRS = Z // 2
    TEACHERS = T * NR
    PROTOS = CL * NP
    GS = loss_scale / student_temp
    names = list(plan(*dims))
    m = Refs()
    for name, ref in zip(names, scratch):
        setattr(m, name, ref)
    send_sem, recv_sem, local_sem = scratch[len(names):]

    load = pltpu.make_async_copy(proto_ref, m.pr, local_sem)
    load.start()

    r = lax.axis_index("rows")
    p = lax.axis_index("protos")
    core = lax.rem(r, 2)
    z = lax.rem(r // 2, Z)
    yl = r // (2 * Z)
    qd = yl * 2 + core

    def row(y_, z_, c_):
        return (y_ * Z + z_) * 2 + c_

    zs = [lax.rem(z + d, Z) for d in range(1, Z)]
    zdev = [(row(yl, z2, core), p) for z2 in zs]
    ps = [lax.rem(p + d, NP) for d in range(1, NP)]
    pdev = [(r, p2) for p2 in ps]
    qs, qdev = [], []
    for d in (1, 2, 3):
        c2 = 1 - core if d & 1 else core
        y2 = 1 - yl if d & 2 else yl
        qs.append(y2 * 2 + c2)
        qdev.append((row(y2, z, c2), p))
    plane = pdev + qdev + [(r2, p2) for r2, _ in qdev for p2 in ps]

    sent = []
    counter = [0]

    def start(copies):
        handles = []
        for src, dst, dev in copies:
            i = counter[0]
            counter[0] += 1
            h = pltpu.make_async_remote_copy(
                src_ref=src, dst_ref=dst, send_sem=send_sem.at[i], recv_sem=recv_sem.at[i],
                device_id=dev, device_id_type=MESH)
            h.start()
            handles.append(h)
            sent.append(h)
        return handles

    def arrive(handles):
        for h in handles:
            h.wait_recv()

    bar = pltpu.get_barrier_semaphore()
    everyone = zdev + plane
    for dev in everyone:
        pl.semaphore_signal(bar, inc=1, device_id=dev, device_id_type=MESH)

    te = tea_ref[...].astype(F32)
    te = (te / jnp.sqrt(jnp.sum(te * te, 1, keepdims=True) + epsilon)).astype(BF)
    m.tp[qd] = te
    m.tq[z] = te
    pl.semaphore_wait(bar, len(everyone))
    c_tp = start([(m.tp.at[qd], m.tp.at[qd], dev) for dev in qdev])

    st = stu_ref[...].astype(F32)
    m.sb[...] = (st / jnp.sqrt(jnp.sum(st * st, 1, keepdims=True) + epsilon)).astype(BF)
    lrf = lay_ref[...].astype(F32)
    lcf = to_col(lrf, S)
    same = (lcf == lrf) & (iota((S, S), 1) < iota((S, S), 0))
    rank = jnp.sum(jnp.where(same, 1.0, 0.0), 1, keepdims=True)
    lc = lcf.astype(jnp.int32)
    zt = lax.rem(lc // 2, Z)
    key = ((lc // (2 * Z)) * 2 + lax.rem(lc, 2)) * Z + zt
    pos = (key * B).astype(F32) + rank
    m.pt[...] = jnp.where(iota((S, S), 1).astype(F32) == pos, 1.0, 0.0)
    idx = (lax.rem(zt, 2) * T).astype(F32) + to_col(pair_ref[...].astype(F32), S)
    m.ssort[...] = dotg(m.pt[...].astype(BF), m.sb[...], TN).astype(BF).reshape(4, S // 4, D)
    isort = jnp.sum(m.pt[...] * idx, 0, keepdims=True)
    spare = jnp.zeros((1, 64), F32)
    for q in range(4):
        m.msort[q] = jnp.concatenate([isort[:, q * 64:(q + 1) * 64], spare], 1)
    m.stu[z, qd] = m.ssort[qd]
    m.meta[z, qd] = m.msort[qd]

    c_meta = start([(m.msort.at[q], m.meta.at[z, qd], dev) for q, dev in zip(qs, qdev)])
    c_stu = start([(m.ssort.at[q], m.stu.at[z, qd], dev) for q, dev in zip(qs, qdev)])
    load.wait()

    def unit(c):
        w = m.pr[:, pl.ds(pl.multiple_of(c, 256), 256)].astype(F32)
        n = jnp.sqrt(jnp.sum(w * w, 0, keepdims=True) + epsilon)
        return w / n, n

    def unit_range(lo, hi):
        @pl.loop(lo, hi)
        def _(i):
            c = pl.multiple_of(i * 256, 256)
            m.w_b[:, pl.ds(c, 256)] = unit(c)[0].astype(BF)

    base = pl.multiple_of(qd * CQ, CQ)
    unit_range(qd * (CQ // 256), (qd + 1) * (CQ // 256))

    arrive(c_tp)
    c_tea = start([(m.tq.at[z], m.tq.at[z], dev) for dev in zdev])

    @pl.loop(0, CQ // 256)
    def _(i):
        c = pl.multiple_of(i * 256, 256)
        e = jnp.exp(dot(m.tp[...].reshape(4 * T, D), m.w_b[:, pl.ds(base + c, 256)]) * (1.0 / teacher_temp))
        m.e8[:, pl.ds(c, 256)] = e
        m.cs[0, :, pl.ds(c, 256)] = jnp.sum(e, 0, keepdims=True)

    c_cs = start([(m.cs.at[0], m.csr.at[0, d], dev) for d, dev in enumerate(zdev)])

    def col_factor(it, c_cs):
        arrive(c_cs)
        total = m.cs[it]
        for d in range(Z - 1):
            total = total + m.csr[it, d]
        return 1.0 / (PROTOS * total)

    def send_rowsum(it):
        acc = jnp.zeros((4 * T, 128), F32)
        for c in range(0, CQ, 256):
            acc = acc + lane_fold(m.e8[:, c:c + 256] * m.va[qd, :, c:c + 256])
        m.rs[it] = to_row(jnp.sum(acc, 1, keepdims=True), 4 * T)
        return start([(m.rs.at[it], m.rsr.at[it, d], dev) for d, dev in enumerate(plane)])

    def row_factor(it, c_rs):
        arrive(c_rs)
        total = m.rs[it]
        for d in range(len(plane)):
            total = total + m.rsr[it, d]
        return 1.0 / (TEACHERS * total)

    zr, zl = lax.rem(z + 1, Z), lax.rem(z + Z - 1, Z)
    right, left = (row(yl, zr, core), p), (row(yl, zl, core), p)
    ring = []

    def ring_step(s):
        if ring:
            arrive(ring[-1])
        a = lax.rem(z + Z - (s - 1), Z)
        b = lax.rem(z + (s - 1), Z)
        if s < Z // 2:
            ring.append(start([(m.stu.at[a], m.stu.at[a], right), (m.stu.at[b], m.stu.at[b], left)]))
        else:
            ring.append(start([
                (m.stu.at[a, pl.ds(0, 2)], m.stu.at[a, pl.ds(0, 2)], right),
                (m.stu.at[b, pl.ds(2, 2)], m.stu.at[b, pl.ds(2, 2)], left)]))

    steps = list(range(1, Z // 2 + 1))

    def next_ring():
        if steps:
            ring_step(steps.pop(0))

    arrive(c_meta)
    arrive(c_stu)
    unit_range(0, qd * (CQ // 256))
    unit_range((qd + 1) * (CQ // 256), CL // 256)

    v1 = col_factor(0, c_cs)
    m.va[qd] = v1
    c_rs = send_rowsum(0)
    next_ring()
    c_metaz = start([(m.meta.at[z], m.meta.at[z], dev) for dev in zdev])

    def a2_step(i, acc):
        c = pl.multiple_of(i * 512, 512)
        a = jnp.exp(dot(m.sb[...], m.w_b[:, pl.ds(c, 512)]) * (1.0 / student_temp))
        m.a2[:, pl.ds(c, 512)] = a
        return acc + lane_fold(a)

    acc = lax.fori_loop(0, CL // 512, a2_step, jnp.zeros((S, 128), F32))
    m.dsrc[...] = to_row(jnp.sum(acc, 1, keepdims=True), S)
    c_den = start([(m.dsrc, m.drecv.at[d], dev) for d, dev in enumerate(pdev)])
    arrive(c_tea)

    for k in range(PAIRS):
        rows = jnp.broadcast_to(m.meta[z], (4, RPR, 128)).reshape(4 * RPR, 128)
        mine = iota((4, RPR, 128), 2) == iota((4, RPR, 128), 1) + k * RPR
        col = jnp.sum(jnp.where(mine.reshape(4 * RPR, 128), rows, 0.0), 1, keepdims=True)
        hot = jnp.where(iota((4 * RPR, 128), 1).astype(F32) == col, 1.0, 0.0).astype(BF)
        got = dot(hot, m.tq[2 * k:2 * k + 2].reshape(2 * T, D)).astype(BF)
        m.tss[:, k * RPR:(k + 1) * RPR, :] = got.reshape(4, RPR, D)
    m.ts[qd] = m.tss[qd]
    c_ts = start([(m.tss.at[q], m.ts.at[qd], dev) for q, dev in zip(qs, qdev)])

    u1 = row_factor(0, c_rs)
    uc1 = to_col(u1, 4 * T)
    for c in range(0, CQ, 256):
        m.cs[1, :, c:c + 256] = jnp.sum(m.e8[:, c:c + 256] * uc1, 0, keepdims=True)
    c_cs = start([(m.cs.at[1], m.csr.at[1, d], dev) for d, dev in enumerate(zdev)])
    next_ring()

    arrive(c_den)
    den = m.dsrc[...]
    for d in range(NP - 1):
        den = den + m.drecv[d]
    sc2 = GS / to_col(den, S)
    scs = jnp.sum(m.pt[...] * sc2, 0, keepdims=True)
    for q in range(4):
        m.dq[q] = jnp.concatenate([scs[:, q * 64:(q + 1) * 64], spare], 1)
    m.dm[z, qd] = m.dq[qd]
    c_dq = start([(m.dq.at[q], m.dm.at[z, qd], dev) for q, dev in zip(qs, qdev)])

    arrive(c_ts)
    m.tsh[...] = dot(m.pt[...].astype(BF), m.ts[...].reshape(S, D)).astype(BF)

    def t2_range(lo, hi):
        @pl.loop(lo, hi)
        def _(i):
            c = pl.multiple_of(i * 512, 512)
            m.t2[:, pl.ds(c, 512)] = jnp.exp(dot(m.tsh[...], m.w_b[:, pl.ds(c, 512)]) * (1.0 / teacher_temp))

    t2_range(0, CL // 512)
    arrive(c_dq)
    c_dz = start([(m.dm.at[z], m.dm.at[z], dev) for dev in zdev])

    v2 = col_factor(1, c_cs)
    m.va[qd] = v2
    c_rs = send_rowsum(1)
    c_va = start([(m.va.at[qd], m.va.at[qd], dev) for dev in qdev])
    next_ring()

    zbase = pl.multiple_of(z * CZ, CZ)

    @pl.loop(0, CZ // 256)
    def _(i):
        c = pl.multiple_of(i * 256, 256)
        w, n = unit(zbase + c)
        m.nz[:, pl.ds(c, 256)] = n
        m.wzf[:, pl.ds(c, 256)] = w
        m.wz[:, pl.ds(c, 256)] = w.astype(BF)

    @pl.loop(0, PAIRS)
    def _(k):
        tk = m.tq[pl.ds(k * 2, 2)].reshape(2 * T, D)
        for c in range(0, CZ, 512):
            e = jnp.exp(dot(tk, m.wz[:, c:c + 512]) * (1.0 / teacher_temp))
            hi = e.astype(BF)
            m.esp[k, 0:128, c:c + 512] = hi
            m.esp[k, 128:256, c:c + 512] = (e - hi.astype(F32)).astype(BF)

    def block_col(ref, k):
        rows = jnp.broadcast_to(ref[...].reshape(NR, 1, 128), (NR, RPR, 128)).reshape(512, 128)
        mine = (iota((NR, RPR, 128), 2) == iota((NR, RPR, 128), 1) + k * RPR).reshape(512, 128)
        return jnp.sum(jnp.where(mine, rows, 0.0), 1, keepdims=True)

    def layout1(k):
        sk = m.stu[:, :, pl.ds(pl.multiple_of(k * RPR, RPR), RPR), :].reshape(512, D)
        m.st[k] = sk.T
        ic = block_col(m.meta, k)
        m.idxc[k] = jnp.broadcast_to(ic, (512, 128))
        sc = block_col(m.dm, k)
        hot = jnp.where(iota((512, 128), 1).astype(F32) == ic, 1.0, 0.0).astype(BF)
        hot = jnp.concatenate([hot, hot], 1)

        @pl.loop(0, CZ // 256)
        def _(i):
            c = pl.multiple_of(i * 256, 256)
            m.a1[k, :, pl.ds(c, 256)] = jnp.exp(dot(sk, m.wz[:, pl.ds(c, 256)]) * (1.0 / student_temp)) * sc
            m.t1[k, :, pl.ds(c, 256)] = dot(hot, m.esp[k, :, pl.ds(c, 256)])

    u2 = row_factor(1, c_rs)
    m.ua[z] = u2 * (GS * TEACHERS)
    c_ua = start([(m.ua.at[z], m.ua.at[z], dev) for dev in zdev])
    while steps:
        next_ring()
    arrive(ring[-1])
    arrive(c_metaz)
    arrive(c_dz)
    for k in range(PAIRS):
        layout1(k)
    arrive(c_va)
    arrive(c_ua)

    def quarter(z_, q):
        return m.ua[z_, :, q * T:(q + 1) * T]

    def own(z_):
        total = None
        for q in range(4):
            one = jnp.where(qd == q, quarter(z_, q), 0.0)
            total = one if total is None else total + one
        return total

    lane = iota((512, 128), 1).astype(F32)
    ucs = []
    for k in range(PAIRS):
        urow = jnp.concatenate([own(2 * k), own(2 * k + 1)], 1)
        ucs.append(jnp.sum(jnp.where(lane == m.idxc[k], jnp.broadcast_to(urow, (512, 128)), 0.0), 1, keepdims=True))

    vbase = pl.multiple_of(lax.rem(z, Z // 4) * CZ, CZ) if Z >= 4 else None

    def v_layout1(c):
        if Z >= 4:
            return m.va[z // (Z // 4), :, pl.ds(pl.multiple_of(vbase + c, 256), 256)]
        per = 4 // Z
        q = z * per + c // CQ
        return m.va[q, :, c % CQ:c % CQ + 256]

    def grad1(h):
        for c in range(h * CH, (h + 1) * CH, 256):
            vv = v_layout1(c)
            total = None
            for k in range(PAIRS):
                g = (m.a1[k, :, c:c + 256] - m.t1[k, :, c:c + 256] * vv * ucs[k]).astype(BF)
                one = dot(m.st[k], g)
                total = one if total is None else total + one
            at = c - h * CH
            m.ins[h, :, at:at + 256] = jnp.sum(m.wzf[:, c:c + 256] * total, 0, keepdims=True)
            for y_ in range(2):
                for z_ in range(Z):
                    for c_ in range(2):
                        f = ((y_ * Z + z_) * 2 + c_) * FB
                        m.gw[h, c_, y_, z_, :, at:at + 256] = total[f:f + FB, :]
        return (start([(m.gw.at[h, 1 - core], m.gwr.at[h], qdev[0])]),
                start([(m.ins.at[h], m.inr.at[h, d], dev) for d, dev in enumerate(qdev)]))

    c_gw, c_in, c_gy, c_gp = [None] * 2, [None] * 2, [None] * 2, [None] * 2
    for h in range(2):
        c_gw[h], c_in[h] = grad1(h)

    def to_y(h):
        arrive(c_gw[h])
        m.gy[h] = m.gw[h, core, 1 - yl] + m.gwr[h, 1 - yl]
        c_gy[h] = start([(m.gy.at[h], m.gyr.at[h], qdev[1])])

    to_y(0)

    usort = []
    for q in range(4):
        for z_ in range(Z):
            usort.append(jnp.broadcast_to(quarter(z_, q), (B, T)))
    usort = jnp.concatenate(usort, 0)
    prow = m.msort[0][:, 0:64]
    for q in range(1, 4):
        prow = jnp.concatenate([prow, m.msort[q][:, 0:64]], 1)
    ztrow = jnp.broadcast_to(lax.rem(lax.broadcasted_iota(jnp.int32, (1, S), 1) // B, 2).astype(F32) * T, (1, S))
    pcol = to_col(prow - ztrow, S)
    ucol = jnp.sum(jnp.where(iota((S, T), 1).astype(F32) == pcol, usort, 0.0), 1, keepdims=True)
    ucol = jnp.sum(m.pt[...] * to_row(ucol, S), 1, keepdims=True)

    def g2_step(i, acc):
        c = pl.multiple_of(i * 512, 512)
        q = (i * 512) // CQ
        w = min(512, CQ)
        if CQ >= 512:
            vv = m.va[q, :, pl.ds(pl.multiple_of(c - q * CQ, 512), 512)]
        else:
            vv = jnp.concatenate([m.va[q + j] for j in range(512 // CQ)], 1)
        g = (m.a2[:, pl.ds(c, 512)] * sc2 - m.t2[:, pl.ds(c, 512)] * vv * ucol).astype(BF)
        return acc + dotg(g, m.w_b[:, pl.ds(c, 512)], NT)

    gsum = lax.fori_loop(0, CL // 1024, g2_step, jnp.zeros((S, D), F32))
    to_y(1)
    gsum = lax.fori_loop(CL // 1024, CL // 512, g2_step, gsum)
    m.gu[...] = gsum.reshape(NP, RB, D)
    c_gu = start([(m.gu.at[p2], m.gur.at[d], dev) for d, (p2, dev) in enumerate(zip(ps, pdev))])

    def to_z(h):
        arrive(c_in[h])
        inner = m.ins[h] + m.inr[h, 0] + m.inr[h, 1] + m.inr[h, 2]
        arrive(c_gy[h])
        inv = 1.0 / m.nz[:, h * CH:(h + 1) * CH]
        for z_ in range(Z):
            f = pl.multiple_of(row(yl, z_, core) * FB, FB)
            mine = m.gw[h, core, yl, z_] + m.gwr[h, yl, z_] + m.gyr[h, z_]
            m.go[h, z_] = (mine - m.wzf[pl.ds(f, FB), h * CH:(h + 1) * CH] * inner) * inv
        m.gpr[h, z] = m.go[h, z]
        c_gp[h] = start([(m.go.at[h, z2], m.gpr.at[h, z], dev) for z2, dev in zip(zs, zdev)])

    to_z(0)
    to_z(1)

    arrive(c_gu)
    gsum = m.gu[p]
    for d in range(NP - 1):
        gsum = gsum + m.gur[d]
    su = stu_ref[pl.ds(pl.multiple_of(p * RB, RB), RB), :].astype(F32)
    un = jnp.sqrt(jnp.sum(su * su, 1, keepdims=True) + epsilon)
    su = su / un
    m.gsr[p] = (gsum - su * jnp.sum(su * gsum, 1, keepdims=True)) / un
    c_gs = start([(m.gsr.at[p], m.gsr.at[p], dev) for dev in pdev])

    for h in range(2):
        arrive(c_gp[h])
        for z_ in range(Z):
            c = z_ * CZ + h * CH
            gp_out[:, c:c + CH] = m.gpr[h, z_]
    arrive(c_gs)
    gs_out[...] = m.gsr[...].reshape(S, D)
    for h in sent:
        h.wait_send()


def body(teacher, students, prototypes, pairing, layout):
    NR = lax.axis_size("rows")
    NP = lax.axis_size("protos")
    T, D = teacher.shape
    S = students.shape[0]
    CL = prototypes.shape[1]
    dims = (NR, NP, T, S, D, CL)
    vmem = pl.BlockSpec(memory_space=pltpu.VMEM)
    scratch = [pltpu.VMEM(shape, dtype) for shape, dtype in plan(*dims).values()]
    scratch += [pltpu.SemaphoreType.DMA((NSEM,)), pltpu.SemaphoreType.DMA((NSEM,)), pltpu.SemaphoreType.DMA]
    return pl.pallas_call(
        functools.partial(kernel, dims),
        out_shape=(
            jax.ShapeDtypeStruct((S, D), F32),
            jax.ShapeDtypeStruct((D // NR, CL), F32),
        ),
        in_specs=[vmem, vmem, pl.BlockSpec(memory_space=pl.ANY), vmem, vmem],
        out_specs=(vmem, vmem),
        scratch_shapes=scratch,
        compiler_params=pltpu.CompilerParams(
            collective_id=0, has_side_effects=True, vmem_limit_bytes=62 * 1024 * 1024
        ),
        name="distill",
    )(teacher, students, prototypes, layout.reshape(1, S), pairing.reshape(1, S))


def solution(mesh):
    in_specs = (P("rows", None), P("rows", None), P(None, "protos"), P("rows"), P("rows"))
    out_specs = (P("rows", None), P("rows", "protos"))
    return jax.shard_map(body, mesh=mesh, in_specs=in_specs, out_specs=out_specs, check_vma=False)
```

time: 88 us -> 83 us (0.943)
  local copies, waits for them, and re-layouts: 6.28 us -> 3.34 us
  Pallas kernels: 80.4 us -> 78.8 us
    reshape x2 -> x0, local copies, waits for them, and re-layouts: 2.95 us -> none  [the longest x1 1.47 us: body(): pairing.reshape(S, 1)]
    pallas_call x1, Pallas kernels: 80.4 us -> 78.8 us  [body(): pl.pallas_call(functools.partial(kernel, dims), out_shape=(jax.ShapeDtype...]
where the time goes in v2:
time: 83 us; the launch traced here: 82.8 us
  Pallas kernels  78.8 us (95%)
  local copies, waits for them, and re-layouts  3.34 us (4%)
    pallas_call x1, Pallas kernels, body(): pl.pallas_call(functools.partial(kernel, dims), out_shape=(jax.ShapeDtype...  78.8 us
    unnamed x2, local copies, waits for them, and re-layouts  3.34 us

profile of v2, /device:TPU:1, one launch (start us, length us, event | category | flops | bytes accessed | tf_op | source)
XLA Modules:
  0.0 82.8 jit_solution(13560206038628296666)
XLA Ops:
  0.6 78.8 %distill.1 = (f32[256,256]{1,0:T(8,128)}, f32[8,8192]{1,0:T(8,128)}) custom-call(bf16[64,256]{1,0:T(8,128)(2,1)} %tea_ref.1, bf16[256,256]{1,0:T(8,128)(2,1)} %stu_ref.1, bf16[256,8192]{1,0:T(8,128)(2,1)} %proto_ref.1, s32[1,256]{1,0:T(1,128)} %bitcast.2, s32[1,256]{1,0:T(1,128)} %bitcast.3), custom_call_target="tpu_custom_call" | custom-call | tf_op jit(solution)/shard_map/distill/pallas_call | solution.py:537
  79.5 1.7 %copy.9 = f32[256,256]{1,0:T(8,128)} copy(f32[256,256]{1,0:T(8,128)} %get-tuple-element.4) | data formatting | bytes 524288
  81.1 1.7 %copy.10 = f32[8,8192]{1,0:T(8,128)} copy(f32[8,8192]{1,0:T(8,128)} %get-tuple-element.5) | data formatting | bytes 524288

commit v3 on v2

--- a/solution.py
+++ b/solution.py
@@ -184,24 +184,49 @@
         pl.semaphore_signal(bar, inc=1, device_id=dev, device_id_type=MESH)
 
     te = tea_ref[...].astype(F32)
-    te = (te / jnp.sqrt(jnp.sum(te * te, 1, keepdims=True) + epsilon)).astype(BF)
+    te = (te * (1.0 / jnp.sqrt(jnp.sum(te * te, 1, keepdims=True) + epsilon))).astype(BF)
     m.tp[qd] = te
     m.tq[z] = te
     pl.semaphore_wait(bar, len(everyone))
     c_tp = start([(m.tp.at[qd], m.tp.at[qd], dev) for dev in qdev])
 
+    load.wait()
+
+    def unit(c):
+        w = m.pr[:, pl.ds(pl.multiple_of(c, 256), 256)].astype(F32)
+        n = jnp.sqrt(jnp.sum(w * w, 0, keepdims=True) + epsilon)
+        return w * (1.0 / n), n
+
+    def unit_range(lo, hi):
+        @pl.loop(lo, hi)
+        def _(i):
+            c = pl.multiple_of(i * 256, 256)
+            m.w_b[:, pl.ds(c, 256)] = unit(c)[0].astype(BF)
+
+    base = pl.multiple_of(qd * CQ, CQ)
+    unit_range(qd * (CQ // 256), (qd + 1) * (CQ // 256))
+
+    arrive(c_tp)
+
+    @pl.loop(0, CQ // 256)
+    def _(i):
+        c = pl.multiple_of(i * 256, 256)
+        e = jnp.exp(dot(m.tp[...].reshape(4 * T, D), m.w_b[:, pl.ds(base + c, 256)]) * (1.0 / teacher_temp))
+        m.e8[:, pl.ds(c, 256)] = e
+        m.cs[0, :, pl.ds(c, 256)] = jnp.sum(e, 0, keepdims=True)
+
+    c_cs = start([(m.cs.at[0], m.csr.at[0, d], dev) for d, dev in enumerate(zdev)])
+    c_tea = start([(m.tq.at[z], m.tq.at[z], dev) for dev in zdev])
     st = stu_ref[...].astype(F32)
-    m.sb[...] = (st / jnp.sqrt(jnp.sum(st * st, 1, keepdims=True) + epsilon)).astype(BF)
-    lrf = lay_ref[...].astype(F32)
-    lcf = to_col(lrf, S)
-    same = (lcf == lrf) & (iota((S, S), 1) < iota((S, S), 0))
-    rank = jnp.sum(jnp.where(same, 1.0, 0.0), 1, keepdims=True)
-    lc = lcf.astype(jnp.int32)
-    zt = lax.rem(lc // 2, Z)
-    key = ((lc // (2 * Z)) * 2 + lax.rem(lc, 2)) * Z + zt
-    pos = (key * B).astype(F32) + rank
+    m.sb[...] = (st * (1.0 / jnp.sqrt(jnp.sum(st * st, 1, keepdims=True) + epsilon))).astype(BF)
+    lay = lay_ref[...]
+    zt = (lay >> 1) & (Z - 1)
+    key = (((lay >> (Z.bit_length())) * 2 + (lay & 1)) * Z + zt).astype(F32)
+    kcol = to_col(key, S)
+    same = (kcol == key) & (iota((S, S), 1) < iota((S, S), 0))
+    pos = kcol * B + jnp.sum(jnp.where(same, 1.0, 0.0), 1, keepdims=True)
     m.pt[...] = jnp.where(iota((S, S), 1).astype(F32) == pos, 1.0, 0.0)
-    idx = (lax.rem(zt, 2) * T).astype(F32) + to_col(pair_ref[...].astype(F32), S)
+    idx = to_col(((zt & 1) * T + pair_ref[...]).astype(F32), S)
     m.ssort[...] = dotg(m.pt[...].astype(BF), m.sb[...], TN).astype(BF).reshape(4, S // 4, D)
     isort = jnp.sum(m.pt[...] * idx, 0, keepdims=True)
     spare = jnp.zeros((1, 64), F32)
@@ -212,33 +237,6 @@
 
     c_meta = start([(m.msort.at[q], m.meta.at[z, qd], dev) for q, dev in zip(qs, qdev)])
     c_stu = start([(m.ssort.at[q], m.stu.at[z, qd], dev) for q, dev in zip(qs, qdev)])
-    load.wait()
-
-    def unit(c):
-        w = m.pr[:, pl.ds(pl.multiple_of(c, 256), 256)].astype(F32)
-        n = jnp.sqrt(jnp.sum(w * w, 0, keepdims=True) + epsilon)
-        return w / n, n
-
-    def unit_range(lo, hi):
-        @pl.loop(lo, hi)
-        def _(i):
-            c = pl.multiple_of(i * 256, 256)
-            m.w_b[:, pl.ds(c, 256)] = unit(c)[0].astype(BF)
-
-    base = pl.multiple_of(qd * CQ, CQ)
-    unit_range(qd * (CQ // 256), (qd + 1) * (CQ // 256))
-
-    arrive(c_tp)
-    c_tea = start([(m.tq.at[z], m.tq.at[z], dev) for dev in zdev])
-
-    @pl.loop(0, CQ // 256)
-    def _(i):
-        c = pl.multiple_of(i * 256, 256)
-        e = jnp.exp(dot(m.tp[...].reshape(4 * T, D), m.w_b[:, pl.ds(base + c, 256)]) * (1.0 / teacher_temp))
-        m.e8[:, pl.ds(c, 256)] = e
-        m.cs[0, :, pl.ds(c, 256)] = jnp.sum(e, 0, keepdims=True)
-
-    c_cs = start([(m.cs.at[0], m.csr.at[0, d], dev) for d, dev in enumerate(zdev)])
 
     def col_factor(it, c_cs):
         arrive(c_cs)
@@ -283,14 +281,14 @@
         if steps:
             ring_step(steps.pop(0))
 
-    arrive(c_meta)
-    arrive(c_stu)
     unit_range(0, qd * (CQ // 256))
     unit_range((qd + 1) * (CQ // 256), CL // 256)
 
     v1 = col_factor(0, c_cs)
     m.va[qd] = v1
     c_rs = send_rowsum(0)
+    arrive(c_meta)
+    arrive(c_stu)
     next_ring()
     c_metaz = start([(m.meta.at[z], m.meta.at[z], dev) for dev in zdev])
 
@@ -314,6 +312,16 @@
         m.tss[:, k * RPR:(k + 1) * RPR, :] = got.reshape(4, RPR, D)
     m.ts[qd] = m.tss[qd]
     c_ts = start([(m.tss.at[q], m.ts.at[qd], dev) for q, dev in zip(qs, qdev)])
+
+    zbase = pl.multiple_of(z * CZ, CZ)
+
+    @pl.loop(0, CZ // 256)
+    def _(i):
+        c = pl.multiple_of(i * 256, 256)
+        w, n = unit(zbase + c)
+        m.nz[:, pl.ds(c, 256)] = n
+        m.wzf[:, pl.ds(c, 256)] = w
+        m.wz[:, pl.ds(c, 256)] = w.astype(BF)
 
     u1 = row_factor(0, c_rs)
     uc1 = to_col(u1, 4 * T)
@@ -350,17 +358,8 @@
     m.va[qd] = v2
     c_rs = send_rowsum(1)
     c_va = start([(m.va.at[qd], m.va.at[qd], dev) for dev in qdev])
-    next_ring()
-
-    zbase = pl.multiple_of(z * CZ, CZ)
-
-    @pl.loop(0, CZ // 256)
-    def _(i):
-        c = pl.multiple_of(i * 256, 256)
-        w, n = unit(zbase + c)
-        m.nz[:, pl.ds(c, 256)] = n
-        m.wzf[:, pl.ds(c, 256)] = w
-        m.wz[:, pl.ds(c, 256)] = w.astype(BF)
+    while steps:
+        next_ring()
 
     @pl.loop(0, PAIRS)
     def _(k):
@@ -376,6 +375,15 @@
         mine = (iota((NR, RPR, 128), 2) == iota((NR, RPR, 128), 1) + k * RPR).reshape(512, 128)
         return jnp.sum(jnp.where(mine, rows, 0.0), 1, keepdims=True)
 
+    vbase = pl.multiple_of(lax.rem(z, Z // 4) * CZ, CZ) if Z >= 4 else None
+
+    def v_layout1(c):
+        if Z >= 4:
+            return m.va[z // (Z // 4), :, pl.ds(pl.multiple_of(vbase + c, 256), 256)]
+        per = 4 // Z
+        q = z * per + c // CQ
+        return m.va[q, :, pl.ds(pl.multiple_of(c % CQ, 256), 256)]
+
     def layout1(k):
         sk = m.stu[:, :, pl.ds(pl.multiple_of(k * RPR, RPR), RPR), :].reshape(512, D)
         m.st[k] = sk.T
@@ -389,19 +397,19 @@
         def _(i):
             c = pl.multiple_of(i * 256, 256)
             m.a1[k, :, pl.ds(c, 256)] = jnp.exp(dot(sk, m.wz[:, pl.ds(c, 256)]) * (1.0 / student_temp)) * sc
-            m.t1[k, :, pl.ds(c, 256)] = dot(hot, m.esp[k, :, pl.ds(c, 256)])
-
+            m.t1[k, :, pl.ds(c, 256)] = dot(hot, m.esp[k, :, pl.ds(c, 256)]) * v_layout1(c)
+
+    arrive(c_va)
+    arrive(c_metaz)
+    arrive(c_dz)
+    arrive(ring[-1])
+    for k in range(PAIRS // 2):
+        layout1(k)
     u2 = row_factor(1, c_rs)
     m.ua[z] = u2 * (GS * TEACHERS)
     c_ua = start([(m.ua.at[z], m.ua.at[z], dev) for dev in zdev])
-    while steps:
-        next_ring()
-    arrive(ring[-1])
-    arrive(c_metaz)
-    arrive(c_dz)
-    for k in range(PAIRS):
+    for k in range(PAIRS // 2, PAIRS):
         layout1(k)
-    arrive(c_va)
     arrive(c_ua)
 
     def quarter(z_, q):
@@ -420,21 +428,11 @@
         urow = jnp.concatenate([own(2 * k), own(2 * k + 1)], 1)
         ucs.append(jnp.sum(jnp.where(lane == m.idxc[k], jnp.broadcast_to(urow, (512, 128)), 0.0), 1, keepdims=True))
 
-    vbase = pl.multiple_of(lax.rem(z, Z // 4) * CZ, CZ) if Z >= 4 else None
-
-    def v_layout1(c):
-        if Z >= 4:
-            return m.va[z // (Z // 4), :, pl.ds(pl.multiple_of(vbase + c, 256), 256)]
-        per = 4 // Z
-        q = z * per + c // CQ
-        return m.va[q, :, c % CQ:c % CQ + 256]
-
     def grad1(h):
         for c in range(h * CH, (h + 1) * CH, 256):
-            vv = v_layout1(c)
             total = None
             for k in range(PAIRS):
-                g = (m.a1[k, :, c:c + 256] - m.t1[k, :, c:c + 256] * vv * ucs[k]).astype(BF)
+                g = (m.a1[k, :, c:c + 256] - m.t1[k, :, c:c + 256] * ucs[k]).astype(BF)
                 one = dot(m.st[k], g)
                 total = one if total is None else total + one
             at = c - h * CH
@@ -466,7 +464,7 @@
     prow = m.msort[0][:, 0:64]
     for q in range(1, 4):
         prow = jnp.concatenate([prow, m.msort[q][:, 0:64]], 1)
-    ztrow = jnp.broadcast_to(lax.rem(lax.broadcasted_iota(jnp.int32, (1, S), 1) // B, 2).astype(F32) * T, (1, S))
+    ztrow = jnp.broadcast_to(((iota((1, S), 1) >> (B.bit_length() - 1)) & 1).astype(F32) * T, (1, S))
     pcol = to_col(prow - ztrow, S)
     ucol = jnp.sum(jnp.where(iota((S, T), 1).astype(F32) == pcol, usort, 0.0), 1, keepdims=True)
     ucol = jnp.sum(m.pt[...] * to_row(ucol, S), 1, keepdims=True)

time: 83 us -> 80.9 us (0.975)
  Pallas kernels: 78.8 us -> 76.7 us
    pallas_call x1, Pallas kernels: 78.8 us -> 76.7 us  [body(): pl.pallas_call(functools.partial(kernel, dims), out_shape=(jax.ShapeDtype...]
where the time goes in v3:
time: 80.9 us; the launch traced here: 80.7 us
  Pallas kernels  76.7 us (95%)
  local copies, waits for them, and re-layouts  3.34 us (4%)
    pallas_call x1, Pallas kernels, body(): pl.pallas_call(functools.partial(kernel, dims), out_shape=(jax.ShapeDtype...  76.7 us
    unnamed x2, local copies, waits for them, and re-layouts  3.34 us

profile of v3, /device:TPU:1, one launch (start us, length us, event | category | flops | bytes accessed | tf_op | source)
XLA Modules:
  0.0 80.7 jit_solution(16458286666680154302)
XLA Ops:
  0.6 76.7 %distill.1 = (f32[256,256]{1,0:T(8,128)}, f32[8,8192]{1,0:T(8,128)}) custom-call(bf16[64,256]{1,0:T(8,128)(2,1)} %tea_ref.1, bf16[256,256]{1,0:T(8,128)(2,1)} %stu_ref.1, bf16[256,8192]{1,0:T(8,128)(2,1)} %proto_ref.1, s32[1,256]{1,0:T(1,128)} %bitcast.2, s32[1,256]{1,0:T(1,128)} %bitcast.3), custom_call_target="tpu_custom_call" | custom-call | tf_op jit(solution)/shard_map/distill/pallas_call | solution.py:535
  77.4 1.7 %copy.9 = f32[256,256]{1,0:T(8,128)} copy(f32[256,256]{1,0:T(8,128)} %get-tuple-element.4) | data formatting | bytes 524288
  79.1 1.7 %copy.10 = f32[8,8192]{1,0:T(8,128)} copy(f32[8,8192]{1,0:T(8,128)} %get-tuple-element.5) | data formatting | bytes 524288

commit v4 on v3

--- a/solution.py
+++ b/solution.py
@@ -61,7 +61,11 @@
     RB = S // NP
     PLANE = 4 * NP - 1
     shapes = dict(
-        pr=((D, CL), BF),
+        w_b=((D, CL), BF),
+        tea=((T, D), BF),
+        stu_in=((S, D), BF),
+        lay=((1, S), jnp.int32),
+        pair=((1, S), jnp.int32),
         tp=((4, T, D), BF),
         tq=((Z, T, D), BF),
         sb=((S, D), BF),
@@ -70,7 +74,6 @@
         msort=((4, 1, 128), F32),
         stu=((Z, 4, S // 4, D), BF),
         meta=((Z, 4, 1, 128), F32),
-        w_b=((D, CL), BF),
         wzf=((D, CZ), F32),
         wz=((D, CZ), BF),
         nz=((1, CZ), F32),
@@ -111,9 +114,10 @@
 
 
 NSEM = 192
-
-
-def kernel(dims, tea_ref, stu_ref, proto_ref, lay_ref, pair_ref, gs_out, gp_out, *scratch):
+VMEM_MIB = 52
+
+
+def kernel(dims, tea_in, stu_in, proto_ref, lay_in, pair_in, gs_out, gp_out, *scratch):
     NR, NP, T, S, D, CL = dims
     Z = NR // 4
     CZ = CL // Z
@@ -132,8 +136,14 @@
     for name, ref in zip(names, scratch):
         setattr(m, name, ref)
     send_sem, recv_sem, local_sem = scratch[len(names):]
-
-    load = pltpu.make_async_copy(proto_ref, m.pr, local_sem)
+    tea_ref, stu_ref, lay_ref, pair_ref = m.tea, m.stu_in, m.lay, m.pair
+
+    load = pltpu.make_async_copy(proto_ref, m.w_b, local_sem.at[0])
+    small = [
+        pltpu.make_async_copy(src, dst, local_sem.at[1 + i])
+        for i, (src, dst) in enumerate(((tea_in, tea_ref), (stu_in, stu_ref), (lay_in, lay_ref), (pair_in, pair_ref)))]
+    for c in small:
+        c.start()
     load.start()
 
     r = lax.axis_index("rows")
@@ -183,6 +193,8 @@
     for dev in everyone:
         pl.semaphore_signal(bar, inc=1, device_id=dev, device_id_type=MESH)
 
+    for c in small:
+        c.wait()
     te = tea_ref[...].astype(F32)
     te = (te * (1.0 / jnp.sqrt(jnp.sum(te * te, 1, keepdims=True) + epsilon))).astype(BF)
     m.tp[qd] = te
@@ -190,33 +202,6 @@
     pl.semaphore_wait(bar, len(everyone))
     c_tp = start([(m.tp.at[qd], m.tp.at[qd], dev) for dev in qdev])
 
-    load.wait()
-
-    def unit(c):
-        w = m.pr[:, pl.ds(pl.multiple_of(c, 256), 256)].astype(F32)
-        n = jnp.sqrt(jnp.sum(w * w, 0, keepdims=True) + epsilon)
-        return w * (1.0 / n), n
-
-    def unit_range(lo, hi):
-        @pl.loop(lo, hi)
-        def _(i):
-            c = pl.multiple_of(i * 256, 256)
-            m.w_b[:, pl.ds(c, 256)] = unit(c)[0].astype(BF)
-
-    base = pl.multiple_of(qd * CQ, CQ)
-    unit_range(qd * (CQ // 256), (qd + 1) * (CQ // 256))
-
-    arrive(c_tp)
-
-    @pl.loop(0, CQ // 256)
-    def _(i):
-        c = pl.multiple_of(i * 256, 256)
-        e = jnp.exp(dot(m.tp[...].reshape(4 * T, D), m.w_b[:, pl.ds(base + c, 256)]) * (1.0 / teacher_temp))
-        m.e8[:, pl.ds(c, 256)] = e
-        m.cs[0, :, pl.ds(c, 256)] = jnp.sum(e, 0, keepdims=True)
-
-    c_cs = start([(m.cs.at[0], m.csr.at[0, d], dev) for d, dev in enumerate(zdev)])
-    c_tea = start([(m.tq.at[z], m.tq.at[z], dev) for dev in zdev])
     st = stu_ref[...].astype(F32)
     m.sb[...] = (st * (1.0 / jnp.sqrt(jnp.sum(st * st, 1, keepdims=True) + epsilon))).astype(BF)
     lay = lay_ref[...]
@@ -238,6 +223,42 @@
     c_meta = start([(m.msort.at[q], m.meta.at[z, qd], dev) for q, dev in zip(qs, qdev)])
     c_stu = start([(m.ssort.at[q], m.stu.at[z, qd], dev) for q, dev in zip(qs, qdev)])
 
+    load.wait()
+
+    def unit(c):
+        w = m.w_b[:, pl.ds(pl.multiple_of(c, 256), 256)].astype(F32)
+        n = jnp.sqrt(jnp.sum(w * w, 0, keepdims=True) + epsilon)
+        return w * (1.0 / n), n
+
+    def unit_range(lo, hi):
+        @pl.loop(lo, hi)
+        def _(i):
+            c = pl.multiple_of(i * 256, 256)
+            m.w_b[:, pl.ds(c, 256)] = unit(c)[0].astype(BF)
+
+    zbase = pl.multiple_of(z * CZ, CZ)
+
+    @pl.loop(0, CZ // 256)
+    def _(i):
+        c = pl.multiple_of(i * 256, 256)
+        w, n = unit(zbase + c)
+        m.nz[:, pl.ds(c, 256)] = n
+        m.wzf[:, pl.ds(c, 256)] = w
+        m.wz[:, pl.ds(c, 256)] = w.astype(BF)
+
+    base = pl.multiple_of(qd * CQ, CQ)
+    unit_range(qd * (CQ // 256), (qd + 1) * (CQ // 256))
+
+    arrive(c_tp)
+
+    @pl.loop(0, CQ // 256)
+    def _(i):
+        c = pl.multiple_of(i * 256, 256)
+        e = jnp.exp(dot(m.tp[...].reshape(4 * T, D), m.w_b[:, pl.ds(base + c, 256)]) * (1.0 / teacher_temp))
+        m.e8[:, pl.ds(c, 256)] = e
+        m.cs[0, :, pl.ds(c, 256)] = jnp.sum(e, 0, keepdims=True)
+
+    c_cs = start([(m.cs.at[0], m.csr.at[0, d], dev) for d, dev in enumerate(zdev)])
     def col_factor(it, c_cs):
         arrive(c_cs)
         total = m.cs[it]
@@ -281,15 +302,17 @@
         if steps:
             ring_step(steps.pop(0))
 
+    arrive(c_meta)
+    arrive(c_stu)
+    next_ring()
     unit_range(0, qd * (CQ // 256))
     unit_range((qd + 1) * (CQ // 256), CL // 256)
 
     v1 = col_factor(0, c_cs)
     m.va[qd] = v1
     c_rs = send_rowsum(0)
-    arrive(c_meta)
-    arrive(c_stu)
     next_ring()
+    c_tea = start([(m.tq.at[z], m.tq.at[z], dev) for dev in zdev])
     c_metaz = start([(m.meta.at[z], m.meta.at[z], dev) for dev in zdev])
 
     def a2_step(i, acc):
@@ -313,22 +336,11 @@
     m.ts[qd] = m.tss[qd]
     c_ts = start([(m.tss.at[q], m.ts.at[qd], dev) for q, dev in zip(qs, qdev)])
 
-    zbase = pl.multiple_of(z * CZ, CZ)
-
-    @pl.loop(0, CZ // 256)
-    def _(i):
-        c = pl.multiple_of(i * 256, 256)
-        w, n = unit(zbase + c)
-        m.nz[:, pl.ds(c, 256)] = n
-        m.wzf[:, pl.ds(c, 256)] = w
-        m.wz[:, pl.ds(c, 256)] = w.astype(BF)
-
     u1 = row_factor(0, c_rs)
     uc1 = to_col(u1, 4 * T)
     for c in range(0, CQ, 256):
         m.cs[1, :, c:c + 256] = jnp.sum(m.e8[:, c:c + 256] * uc1, 0, keepdims=True)
     c_cs = start([(m.cs.at[1], m.csr.at[1, d], dev) for d, dev in enumerate(zdev)])
-    next_ring()
 
     arrive(c_den)
     den = m.dsrc[...]
@@ -341,6 +353,7 @@
     m.dm[z, qd] = m.dq[qd]
     c_dq = start([(m.dq.at[q], m.dm.at[z, qd], dev) for q, dev in zip(qs, qdev)])
 
+    next_ring()
     arrive(c_ts)
     m.tsh[...] = dot(m.pt[...].astype(BF), m.ts[...].reshape(S, D)).astype(BF)
 
@@ -446,15 +459,12 @@
                 start([(m.ins.at[h], m.inr.at[h, d], dev) for d, dev in enumerate(qdev)]))
 
     c_gw, c_in, c_gy, c_gp = [None] * 2, [None] * 2, [None] * 2, [None] * 2
-    for h in range(2):
-        c_gw[h], c_in[h] = grad1(h)
+    c_gw[0], c_in[0] = grad1(0)
 
     def to_y(h):
         arrive(c_gw[h])
         m.gy[h] = m.gw[h, core, 1 - yl] + m.gwr[h, 1 - yl]
         c_gy[h] = start([(m.gy.at[h], m.gyr.at[h], qdev[1])])
-
-    to_y(0)
 
     usort = []
     for q in range(4):
@@ -481,10 +491,11 @@
         return acc + dotg(g, m.w_b[:, pl.ds(c, 512)], NT)
 
     gsum = lax.fori_loop(0, CL // 1024, g2_step, jnp.zeros((S, D), F32))
-    to_y(1)
+    to_y(0)
     gsum = lax.fori_loop(CL // 1024, CL // 512, g2_step, gsum)
     m.gu[...] = gsum.reshape(NP, RB, D)
     c_gu = start([(m.gu.at[p2], m.gur.at[d], dev) for d, (p2, dev) in enumerate(zip(ps, pdev))])
+    c_gw[1], c_in[1] = grad1(1)
 
     def to_z(h):
         arrive(c_in[h])
@@ -498,8 +509,8 @@
         m.gpr[h, z] = m.go[h, z]
         c_gp[h] = start([(m.go.at[h, z2], m.gpr.at[h, z], dev) for z2, dev in zip(zs, zdev)])
 
+    to_y(1)
     to_z(0)
-    to_z(1)
 
     arrive(c_gu)
     gsum = m.gu[p]
@@ -511,6 +522,7 @@
     m.gsr[p] = (gsum - su * jnp.sum(su * gsum, 1, keepdims=True)) / un
     c_gs = start([(m.gsr.at[p], m.gsr.at[p], dev) for dev in pdev])
 
+    to_z(1)
     for h in range(2):
         arrive(c_gp[h])
         for z_ in range(Z):
@@ -531,18 +543,18 @@
     dims = (NR, NP, T, S, D, CL)
     vmem = pl.BlockSpec(memory_space=pltpu.VMEM)
     scratch = [pltpu.VMEM(shape, dtype) for shape, dtype in plan(*dims).values()]
-    scratch += [pltpu.SemaphoreType.DMA((NSEM,)), pltpu.SemaphoreType.DMA((NSEM,)), pltpu.SemaphoreType.DMA]
+    scratch += [pltpu.SemaphoreType.DMA((NSEM,)), pltpu.SemaphoreType.DMA((NSEM,)), pltpu.SemaphoreType.DMA((5,))]
     return pl.pallas_call(
         functools.partial(kernel, dims),
         out_shape=(
             jax.ShapeDtypeStruct((S, D), F32),
             jax.ShapeDtypeStruct((D // NR, CL), F32),
         ),
-        in_specs=[vmem, vmem, pl.BlockSpec(memory_space=pl.ANY), vmem, vmem],
+        in_specs=[pl.BlockSpec(memory_space=pl.ANY)] * 5,
         out_specs=(vmem, vmem),
         scratch_shapes=scratch,
         compiler_params=pltpu.CompilerParams(
-            collective_id=0, has_side_effects=True, vmem_limit_bytes=62 * 1024 * 1024
+            collective_id=0, has_side_effects=True, vmem_limit_bytes=VMEM_MIB * 1024 * 1024
         ),
         name="distill",
     )(teacher, students, prototypes, layout.reshape(1, S), pairing.reshape(1, S))

time: 80.9 us -> 83.1 us (1.027)
  Pallas kernels: 76.7 us -> 77.9 us
  local copies, waits for them, and re-layouts: 3.34 us -> 4.42 us
    pallas_call x1, Pallas kernels: 76.7 us -> 77.9 us  [body(): pl.pallas_call(functools.partial(kernel, dims), out_shape=(jax.ShapeDtype...]
    unnamed x2 -> x10, local copies, waits for them, and re-layouts: 3.34 us -> 4.42 us
where the time goes in v4:
time: 83.1 us; the launch traced here: 82.9 us
  Pallas kernels  77.9 us (94%)
  local copies, waits for them, and re-layouts  4.42 us (5%)
    pallas_call x1, Pallas kernels, body(): pl.pallas_call(functools.partial(kernel, dims), out_shape=(jax.ShapeDtype...  77.9 us
    unnamed x10, local copies, waits for them, and re-layouts  4.42 us

profile of v4, /device:TPU:1, one launch (start us, length us, event | category | flops | bytes accessed | tf_op | source)
XLA Modules:
  0.0 82.9 jit_solution(1247588412092172828)
XLA Ops:
  0.6 0.0 copy-start
  0.6 0.9 %copy-done = bf16[256,256]{1,0:T(8,128)(2,1)S(1)} copy-done((bf16[256,256]{1,0:T(8,128)(2,1)S(1)}, bf16[256,256]{1,0:T(8,128)(2,1)}, u32[]{:S(2)}) %copy-start) | copy-done | bytes 131096
  1.5 0.0 copy-start.1
  1.5 0.8 copy-done.1
  2.3 0.0 copy-start.2
  2.3 0.7 copy-done.2
  3.0 0.0 copy-start.3
  3.0 0.7 copy-done.3
  3.7 77.9 %distill.1 = (f32[256,256]{1,0:T(8,128)S(1)}, f32[8,8192]{1,0:T(8,128)S(1)}) custom-call(bf16[64,256]{1,0:T(8,128)(2,1)S(1)} %copy-done.1, bf16[256,256]{1,0:T(8,128)(2,1)S(1)} %copy-done, bf16[256,8192]{1,0:T(8,128)(2,1)} %proto_ref.1, s32[1,256]{1,0:T(1,128)S(1)} %bitcast.2, s32[1,256]{1,0:T(1,128)S(1)} %bitcast.3), custom_call_target="tpu_custom_call" | custom-call | tf_op jit(solution)/shard_map/distill/pallas_call | solution.py:547
  81.5 0.7 copy.9
  82.2 0.7 copy.10
Async XLA Ops:
  0.6 0.9 %copy-start = (bf16[256,256]{1,0:T(8,128)(2,1)S(1)}, bf16[256,256]{1,0:T(8,128)(2,1)}, u32[]{:S(2)}) copy-start(bf16[256,256]{1,0:T(8,128)(2,1)} %stu_in.1) | copy-start | bytes 393220
  1.5 0.8 copy-start.1
  2.3 0.7 copy-start.2
  3.0 0.7 copy-start.3

commit v5 on v4

--- a/solution.py
+++ b/solution.py
@@ -64,8 +64,7 @@
         w_b=((D, CL), BF),
         tea=((T, D), BF),
         stu_in=((S, D), BF),
-        lay=((1, S), jnp.int32),
-        pair=((1, S), jnp.int32),
+        row_of=((1, S), jnp.int32),
         tp=((4, T, D), BF),
         tq=((Z, T, D), BF),
         sb=((S, D), BF),
@@ -113,11 +112,11 @@
     return shapes
 
 
-NSEM = 192
+NSEM = 224
 VMEM_MIB = 52
 
 
-def kernel(dims, tea_in, stu_in, proto_ref, lay_in, pair_in, gs_out, gp_out, *scratch):
+def kernel(dims, tea_in, stu_in, proto_ref, row_in, gs_out, gp_out, *scratch):
     NR, NP, T, S, D, CL = dims
     Z = NR // 4
     CZ = CL // Z
@@ -136,12 +135,12 @@
     for name, ref in zip(names, scratch):
         setattr(m, name, ref)
     send_sem, recv_sem, local_sem = scratch[len(names):]
-    tea_ref, stu_ref, lay_ref, pair_ref = m.tea, m.stu_in, m.lay, m.pair
+    tea_ref, stu_ref, row_ref = m.tea, m.stu_in, m.row_of
 
     load = pltpu.make_async_copy(proto_ref, m.w_b, local_sem.at[0])
     small = [
         pltpu.make_async_copy(src, dst, local_sem.at[1 + i])
-        for i, (src, dst) in enumerate(((tea_in, tea_ref), (stu_in, stu_ref), (lay_in, lay_ref), (pair_in, pair_ref)))]
+        for i, (src, dst) in enumerate(((tea_in, tea_ref), (stu_in, stu_ref), (row_in, row_ref)))]
     for c in small:
         c.start()
     load.start()
@@ -204,14 +203,14 @@
 
     st = stu_ref[...].astype(F32)
     m.sb[...] = (st * (1.0 / jnp.sqrt(jnp.sum(st * st, 1, keepdims=True) + epsilon))).astype(BF)
-    lay = lay_ref[...]
+    lay = row_ref[...] >> (T.bit_length() - 1)
     zt = (lay >> 1) & (Z - 1)
     key = (((lay >> (Z.bit_length())) * 2 + (lay & 1)) * Z + zt).astype(F32)
     kcol = to_col(key, S)
     same = (kcol == key) & (iota((S, S), 1) < iota((S, S), 0))
     pos = kcol * B + jnp.sum(jnp.where(same, 1.0, 0.0), 1, keepdims=True)
     m.pt[...] = jnp.where(iota((S, S), 1).astype(F32) == pos, 1.0, 0.0)
-    idx = to_col(((zt & 1) * T + pair_ref[...]).astype(F32), S)
+    idx = to_col(((zt & 1) * T + (row_ref[...] & (T - 1))).astype(F32), S)
     m.ssort[...] = dotg(m.pt[...].astype(BF), m.sb[...], TN).astype(BF).reshape(4, S // 4, D)
     isort = jnp.sum(m.pt[...] * idx, 0, keepdims=True)
     spare = jnp.zeros((1, 64), F32)
@@ -280,39 +279,21 @@
             total = total + m.rsr[it, d]
         return 1.0 / (TEACHERS * total)
 
-    zr, zl = lax.rem(z + 1, Z), lax.rem(z + Z - 1, Z)
-    right, left = (row(yl, zr, core), p), (row(yl, zl, core), p)
-    ring = []
-
-    def ring_step(s):
-        if ring:
-            arrive(ring[-1])
-        a = lax.rem(z + Z - (s - 1), Z)
-        b = lax.rem(z + (s - 1), Z)
-        if s < Z // 2:
-            ring.append(start([(m.stu.at[a], m.stu.at[a], right), (m.stu.at[b], m.stu.at[b], left)]))
-        else:
-            ring.append(start([
-                (m.stu.at[a, pl.ds(0, 2)], m.stu.at[a, pl.ds(0, 2)], right),
-                (m.stu.at[b, pl.ds(2, 2)], m.stu.at[b, pl.ds(2, 2)], left)]))
-
-    steps = list(range(1, Z // 2 + 1))
-
-    def next_ring():
-        if steps:
-            ring_step(steps.pop(0))
-
+    def send_piece(q):
+        return start([(m.stu.at[z, q], m.stu.at[z, q], dev) for dev in zdev])
+
+    c_tea = start([(m.tq.at[z], m.tq.at[z], dev) for dev in zdev])
+    c_pieces = [send_piece(qd)]
     arrive(c_meta)
     arrive(c_stu)
-    next_ring()
     unit_range(0, qd * (CQ // 256))
     unit_range((qd + 1) * (CQ // 256), CL // 256)
 
     v1 = col_factor(0, c_cs)
     m.va[qd] = v1
     c_rs = send_rowsum(0)
-    next_ring()
-    c_tea = start([(m.tq.at[z], m.tq.at[z], dev) for dev in zdev])
+    c_pieces.append(send_piece(qs[0]))
+    c_pieces.append(send_piece(qs[1]))
     c_metaz = start([(m.meta.at[z], m.meta.at[z], dev) for dev in zdev])
 
     def a2_step(i, acc):
@@ -324,6 +305,13 @@
     acc = lax.fori_loop(0, CL // 512, a2_step, jnp.zeros((S, 128), F32))
     m.dsrc[...] = to_row(jnp.sum(acc, 1, keepdims=True), S)
     c_den = start([(m.dsrc, m.drecv.at[d], dev) for d, dev in enumerate(pdev)])
+
+    u1 = row_factor(0, c_rs)
+    uc1 = to_col(u1, 4 * T)
+    for c in range(0, CQ, 256):
+        m.cs[1, :, c:c + 256] = jnp.sum(m.e8[:, c:c + 256] * uc1, 0, keepdims=True)
+    c_cs = start([(m.cs.at[1], m.csr.at[1, d], dev) for d, dev in enumerate(zdev)])
+    c_pieces.append(send_piece(qs[2]))
     arrive(c_tea)
 
     for k in range(PAIRS):
@@ -335,12 +323,6 @@
         m.tss[:, k * RPR:(k + 1) * RPR, :] = got.reshape(4, RPR, D)
     m.ts[qd] = m.tss[qd]
     c_ts = start([(m.tss.at[q], m.ts.at[qd], dev) for q, dev in zip(qs, qdev)])
-
-    u1 = row_factor(0, c_rs)
-    uc1 = to_col(u1, 4 * T)
-    for c in range(0, CQ, 256):
-        m.cs[1, :, c:c + 256] = jnp.sum(m.e8[:, c:c + 256] * uc1, 0, keepdims=True)
-    c_cs = start([(m.cs.at[1], m.csr.at[1, d], dev) for d, dev in enumerate(zdev)])
 
     arrive(c_den)
     den = m.dsrc[...]
@@ -353,27 +335,6 @@
     m.dm[z, qd] = m.dq[qd]
     c_dq = start([(m.dq.at[q], m.dm.at[z, qd], dev) for q, dev in zip(qs, qdev)])
 
-    next_ring()
-    arrive(c_ts)
-    m.tsh[...] = dot(m.pt[...].astype(BF), m.ts[...].reshape(S, D)).astype(BF)
-
-    def t2_range(lo, hi):
-        @pl.loop(lo, hi)
-        def _(i):
-            c = pl.multiple_of(i * 512, 512)
-            m.t2[:, pl.ds(c, 512)] = jnp.exp(dot(m.tsh[...], m.w_b[:, pl.ds(c, 512)]) * (1.0 / teacher_temp))
-
-    t2_range(0, CL // 512)
-    arrive(c_dq)
-    c_dz = start([(m.dm.at[z], m.dm.at[z], dev) for dev in zdev])
-
-    v2 = col_factor(1, c_cs)
-    m.va[qd] = v2
-    c_rs = send_rowsum(1)
-    c_va = start([(m.va.at[qd], m.va.at[qd], dev) for dev in qdev])
-    while steps:
-        next_ring()
-
     @pl.loop(0, PAIRS)
     def _(k):
         tk = m.tq[pl.ds(k * 2, 2)].reshape(2 * T, D)
@@ -383,6 +344,24 @@
             m.esp[k, 0:128, c:c + 512] = hi
             m.esp[k, 128:256, c:c + 512] = (e - hi.astype(F32)).astype(BF)
 
+    arrive(c_dq)
+    c_dz = start([(m.dm.at[z], m.dm.at[z], dev) for dev in zdev])
+
+    v2 = col_factor(1, c_cs)
+    m.va[qd] = v2
+    c_rs = send_rowsum(1)
+    c_va = start([(m.va.at[qd], m.va.at[qd], dev) for dev in qdev])
+    arrive(c_ts)
+    m.tsh[...] = dot(m.pt[...].astype(BF), m.ts[...].reshape(S, D)).astype(BF)
+
+    def t2_range(lo, hi):
+        @pl.loop(lo, hi)
+        def _(i):
+            c = pl.multiple_of(i * 512, 512)
+            m.t2[:, pl.ds(c, 512)] = jnp.exp(dot(m.tsh[...], m.w_b[:, pl.ds(c, 512)]) * (1.0 / teacher_temp))
+
+    t2_range(0, CL // 512)
+
     def block_col(ref, k):
         rows = jnp.broadcast_to(ref[...].reshape(NR, 1, 128), (NR, RPR, 128)).reshape(512, 128)
         mine = (iota((NR, RPR, 128), 2) == iota((NR, RPR, 128), 1) + k * RPR).reshape(512, 128)
@@ -415,13 +394,14 @@
     arrive(c_va)
     arrive(c_metaz)
     arrive(c_dz)
-    arrive(ring[-1])
-    for k in range(PAIRS // 2):
+    for c in c_pieces:
+        arrive(c)
+    for k in range(PAIRS // 4):
         layout1(k)
     u2 = row_factor(1, c_rs)
     m.ua[z] = u2 * (GS * TEACHERS)
     c_ua = start([(m.ua.at[z], m.ua.at[z], dev) for dev in zdev])
-    for k in range(PAIRS // 2, PAIRS):
+    for k in range(PAIRS // 4, PAIRS):
         layout1(k)
     arrive(c_ua)
 
@@ -550,14 +530,14 @@
             jax.ShapeDtypeStruct((S, D), F32),
             jax.ShapeDtypeStruct((D // NR, CL), F32),
         ),
-        in_specs=[pl.BlockSpec(memory_space=pl.ANY)] * 5,
+        in_specs=[pl.BlockSpec(memory_space=pl.ANY)] * 4,
         out_specs=(vmem, vmem),
         scratch_shapes=scratch,
         compiler_params=pltpu.CompilerParams(
             collective_id=0, has_side_effects=True, vmem_limit_bytes=VMEM_MIB * 1024 * 1024
         ),
         name="distill",
-    )(teacher, students, prototypes, layout.reshape(1, S), pairing.reshape(1, S))
+    )(teacher, students, prototypes, (layout * T + pairing).reshape(1, S))
 
 
 def solution(mesh):

time: 83.1 us -> 87.3 us (1.051)
  Pallas kernels: 77.9 us -> 82.7 us
  local copies, waits for them, and re-layouts: 4.42 us -> 3.07 us
    pallas_call x1, Pallas kernels: 77.9 us -> 82.7 us  [body(): pl.pallas_call(functools.partial(kernel, dims), out_shape=(jax.ShapeDtype...]
    unnamed x10 -> x6, local copies, waits for them, and re-layouts: 4.42 us -> 3.07 us
where the time goes in v5:
time: 87.3 us; the launch traced here: 87.2 us
  Pallas kernels  82.7 us (95%)
  local copies, waits for them, and re-layouts  3.07 us (4%)
    pallas_call x1, Pallas kernels, body(): pl.pallas_call(functools.partial(kernel, dims), out_shape=(jax.ShapeDtype...  82.7 us
    unnamed x6, local copies, waits for them, and re-layouts  3.07 us

profile of v5, /device:TPU:1, one launch (start us, length us, event | category | flops | bytes accessed | tf_op | source)
XLA Modules:
  0.0 87.2 jit_solution(5191540542064652523)
XLA Ops:
  0.6 0.7 multiply_add_fusion
  1.3 0.0 copy-start
  1.3 0.9 %copy-done = bf16[256,256]{1,0:T(8,128)(2,1)S(1)} copy-done((bf16[256,256]{1,0:T(8,128)(2,1)S(1)}, bf16[256,256]{1,0:T(8,128)(2,1)}, u32[]{:S(2)}) %copy-start) | copy-done | bytes 131096
  2.2 0.0 copy-start.1
  2.2 0.8 copy-done.1
  3.0 82.7 %distill.1 = (f32[256,256]{1,0:T(8,128)S(1)}, f32[8,8192]{1,0:T(8,128)S(1)}) custom-call(bf16[64,256]{1,0:T(8,128)(2,1)S(1)} %copy-done.1, bf16[256,256]{1,0:T(8,128)(2,1)S(1)} %copy-done, bf16[256,8192]{1,0:T(8,128)(2,1)} %proto_ref.1, s32[1,256]{1,0:T(1,128)S(1)} %bitcast.1), custom_call_target="tpu_custom_call" | custom-call | tf_op jit(solution)/shard_map/distill/pallas_call | solution.py:527
  85.8 0.7 copy.9
  86.5 0.7 copy.10
Async XLA Ops:
  1.3 0.9 %copy-start = (bf16[256,256]{1,0:T(8,128)(2,1)S(1)}, bf16[256,256]{1,0:T(8,128)(2,1)}, u32[]{:S(2)}) copy-start(bf16[256,256]{1,0:T(8,128)(2,1)} %stu_in.1) | copy-start | bytes 393220
  2.2 0.8 copy-start.1

commit v6 on v4

--- a/solution.py
+++ b/solution.py
@@ -114,7 +114,7 @@
 
 
 NSEM = 192
-VMEM_MIB = 52
+VMEM_MIB = 60
 
 
 def kernel(dims, tea_in, stu_in, proto_ref, lay_in, pair_in, gs_out, gp_out, *scratch):
@@ -201,6 +201,7 @@
     m.tq[z] = te
     pl.semaphore_wait(bar, len(everyone))
     c_tp = start([(m.tp.at[qd], m.tp.at[qd], dev) for dev in qdev])
+    c_tea = start([(m.tq.at[z], m.tq.at[z], dev) for dev in zdev])
 
     st = stu_ref[...].astype(F32)
     m.sb[...] = (st * (1.0 / jnp.sqrt(jnp.sum(st * st, 1, keepdims=True) + epsilon))).astype(BF)
@@ -312,7 +313,6 @@
     m.va[qd] = v1
     c_rs = send_rowsum(0)
     next_ring()
-    c_tea = start([(m.tq.at[z], m.tq.at[z], dev) for dev in zdev])
     c_metaz = start([(m.meta.at[z], m.meta.at[z], dev) for dev in zdev])
 
     def a2_step(i, acc):

time: 83.1 us -> 76.9 us (0.925)
  Pallas kernels: 77.9 us -> 72.4 us
  local copies, waits for them, and re-layouts: 4.42 us -> 3.34 us
    pallas_call x1, Pallas kernels: 77.9 us -> 72.4 us  [body(): pl.pallas_call(functools.partial(kernel, dims), out_shape=(jax.ShapeDtype...]
    unnamed x10 -> x2, local copies, waits for them, and re-layouts: 4.42 us -> 3.34 us
where the time goes in v6:
time: 76.9 us; the launch traced here: 76.4 us
  Pallas kernels  72.4 us (94%)
  local copies, waits for them, and re-layouts  3.34 us (4%)
    pallas_call x1, Pallas kernels, body(): pl.pallas_call(functools.partial(kernel, dims), out_shape=(jax.ShapeDtype...  72.4 us
    unnamed x2, local copies, waits for them, and re-layouts  3.34 us

profile of v6, /device:TPU:1, one launch (start us, length us, event | category | flops | bytes accessed | tf_op | source)
XLA Modules:
  0.0 76.4 jit_solution(2952538583664713842)
XLA Ops:
  0.6 72.4 %distill.1 = (f32[256,256]{1,0:T(8,128)}, f32[8,8192]{1,0:T(8,128)}) custom-call(bf16[64,256]{1,0:T(8,128)(2,1)} %tea_in.1, bf16[256,256]{1,0:T(8,128)(2,1)} %stu_in.1, bf16[256,8192]{1,0:T(8,128)(2,1)} %proto_ref.1, s32[1,256]{1,0:T(1,128)} %bitcast.2, s32[1,256]{1,0:T(1,128)} %bitcast.3), custom_call_target="tpu_custom_call" | custom-call | tf_op jit(solution)/shard_map/distill/pallas_call | solution.py:547
  73.0 1.7 %copy.9 = f32[256,256]{1,0:T(8,128)} copy(f32[256,256]{1,0:T(8,128)} %get-tuple-element.4) | data formatting | bytes 524288
  74.7 1.7 %copy.10 = f32[8,8192]{1,0:T(8,128)} copy(f32[8,8192]{1,0:T(8,128)} %get-tuple-element.5) | data formatting | bytes 524288

commit v7 on v6

--- a/solution.py
+++ b/solution.py
@@ -412,16 +412,14 @@
             m.a1[k, :, pl.ds(c, 256)] = jnp.exp(dot(sk, m.wz[:, pl.ds(c, 256)]) * (1.0 / student_temp)) * sc
             m.t1[k, :, pl.ds(c, 256)] = dot(hot, m.esp[k, :, pl.ds(c, 256)]) * v_layout1(c)
 
+    u2 = row_factor(1, c_rs)
+    m.ua[z] = u2 * (GS * TEACHERS)
+    c_ua = start([(m.ua.at[z], m.ua.at[z], dev) for dev in zdev])
     arrive(c_va)
     arrive(c_metaz)
     arrive(c_dz)
     arrive(ring[-1])
-    for k in range(PAIRS // 2):
-        layout1(k)
-    u2 = row_factor(1, c_rs)
-    m.ua[z] = u2 * (GS * TEACHERS)
-    c_ua = start([(m.ua.at[z], m.ua.at[z], dev) for dev in zdev])
-    for k in range(PAIRS // 2, PAIRS):
+    for k in range(PAIRS):
         layout1(k)
     arrive(c_ua)
 
@@ -460,12 +458,14 @@
 
     c_gw, c_in, c_gy, c_gp = [None] * 2, [None] * 2, [None] * 2, [None] * 2
     c_gw[0], c_in[0] = grad1(0)
+    c_gw[1], c_in[1] = grad1(1)
 
     def to_y(h):
         arrive(c_gw[h])
         m.gy[h] = m.gw[h, core, 1 - yl] + m.gwr[h, 1 - yl]
         c_gy[h] = start([(m.gy.at[h], m.gyr.at[h], qdev[1])])
 
+    to_y(0)
     usort = []
     for q in range(4):
         for z_ in range(Z):
@@ -491,11 +491,10 @@
         return acc + dotg(g, m.w_b[:, pl.ds(c, 512)], NT)
 
     gsum = lax.fori_loop(0, CL // 1024, g2_step, jnp.zeros((S, D), F32))
-    to_y(0)
+    to_y(1)
     gsum = lax.fori_loop(CL // 1024, CL // 512, g2_step, gsum)
     m.gu[...] = gsum.reshape(NP, RB, D)
     c_gu = start([(m.gu.at[p2], m.gur.at[d], dev) for d, (p2, dev) in enumerate(zip(ps, pdev))])
-    c_gw[1], c_in[1] = grad1(1)
 
     def to_z(h):
         arrive(c_in[h])
@@ -509,7 +508,6 @@
         m.gpr[h, z] = m.go[h, z]
         c_gp[h] = start([(m.go.at[h, z2], m.gpr.at[h, z], dev) for z2, dev in zip(zs, zdev)])
 
-    to_y(1)
     to_z(0)
 
     arrive(c_gu)

time: 76.9 us -> 75.8 us (0.986)
  no operation moved by 1% of the time
where the time goes in v7:
time: 75.8 us; the launch traced here: 75.7 us
  Pallas kernels  71.7 us (95%)
  local copies, waits for them, and re-layouts  3.34 us (4%)
    pallas_call x1, Pallas kernels, body(): pl.pallas_call(functools.partial(kernel, dims), out_shape=(jax.ShapeDtype...  71.7 us
    unnamed x2, local copies, waits for them, and re-layouts  3.34 us

profile of v7, /device:TPU:1, one launch (start us, length us, event | category | flops | bytes accessed | tf_op | source)
XLA Modules:
  0.0 75.7 jit_solution(516992161725541736)
XLA Ops:
  0.6 71.7 %distill.1 = (f32[256,256]{1,0:T(8,128)}, f32[8,8192]{1,0:T(8,128)}) custom-call(bf16[64,256]{1,0:T(8,128)(2,1)} %tea_in.1, bf16[256,256]{1,0:T(8,128)(2,1)} %stu_in.1, bf16[256,8192]{1,0:T(8,128)(2,1)} %proto_ref.1, s32[1,256]{1,0:T(1,128)} %bitcast.2, s32[1,256]{1,0:T(1,128)} %bitcast.3), custom_call_target="tpu_custom_call" | custom-call | tf_op jit(solution)/shard_map/distill/pallas_call | solution.py:545
  72.4 1.7 %copy.9 = f32[256,256]{1,0:T(8,128)} copy(f32[256,256]{1,0:T(8,128)} %get-tuple-element.4) | data formatting | bytes 524288
  74.0 1.7 %copy.10 = f32[8,8192]{1,0:T(8,128)} copy(f32[8,8192]{1,0:T(8,128)} %get-tuple-element.5) | data formatting | bytes 524288
